TPU v7x, 32 devices: a whole 2x2x4 slice. The times are simulated.
32 devices in a mesh: view: 8 (over y, x, core), band: 4 (over z).
Axes of the slice: x: 2, y: 2, z: 4, core: 2. Of those that a mesh axis runs over, the one named last changes fastest.
Arguments:
- gaussians: float32 [512, 62, 256], P(('view', 'band')), may hold values from -8 to 128, as said below
- first_moment: float32 [512, 62, 256], P(('view', 'band')), may hold values from -0.6 to 0.6
- second_moment: float32 [512, 62, 256], P(('view', 'band')), may hold values from 0.0001 to 0.1
- camera: float32 [8, 9], P('view'), may hold values from -352 to 352, as said below
- target: float32 [8, 3, 64, 128], P('view', None, 'band'), may hold values from 0 to 1
- block_list: int32 [8, 4, 16], P('view', 'band'), may hold values from -1 to 511, as said below
- block_count: int32 [8, 4], P('view', 'band'), may hold values from 12 to 16, as said below
- tile_start: int32 [8, 4, 8], P('view', 'band'), may hold values from 0 to 15, as said below
- tile_end: int32 [8, 4, 8], P('view', 'band'), may hold values from 1 to 16, as said below
Outputs:
- new_gaussians: float32 [512, 62, 256], P(('view', 'band'))
- new_first_moment: float32 [512, 62, 256], P(('view', 'band'))
- new_second_moment: float32 [512, 62, 256], P(('view', 'band'))
- mean_loss: float32 [], replicated
- grads: float32 [512, 62, 256], P(('view', 'band'))
Inputs may be any that keep to these rules, and one draw needn't show every extreme that they name: Block k is held by device k // 16, devices counted with view slowest. Entry i of block_list[v, b] is a block for i < block_count[v, b] and -1 after; the live entries of one band are distinct, at most 1 of them are held by one device, and in every band some device holds exactly 1 of them. `block_count`: some band has exactly 16. tile_start < tile_end <= block_count of the band; tile_end - tile_start is at most 2, and exactly 2 for some tile of every band; the tiles of a band together cover every live position. `tile_end`: see tile_start. `gaussians`: component 9 of every Gaussian lies in [1, 2]; components 6 to 8 lie in [0, 2]. `camera`: A0 x A1 has a third entry of 0.6 or more.
All inputs are finite; a program needn't handle non-finite values.
Results may differ from a plain program's by a relative error of at most 0.0003.
Values sent between devices are 32-bit elements; how exact they have to be, the bound alone decides.
A program may use at most 128 MiB of HBM per device.

v0:
```python
import functools
import math

import jax
import jax.numpy as jnp
import numpy as np
from jax import lax
from jax.experimental import pallas as pl
from jax.experimental.pallas import tpu as pltpu
from jax.sharding import PartitionSpec as P

TILE = 16
TILE_MOST = 2
HALO = 5
REACH = 2 * HALO
ROW_REC = 9
GEO_REC = 6
PIECES = 4

HIGHEST_MODE = lax.Precision.HIGHEST
SSIM_WEIGHT = 0.2
ABS_WEIGHT = 0.8
STAB_MEAN = 0.0001
STAB_VAR = 0.0009
BIAS_FIRST = 1.0 - math.exp(100.0 * math.log(0.9))
BIAS_SECOND = 1.0 - math.exp(100.0 * math.log(0.999))
LOG2_E = math.log2(math.e)
SH_ZERO = 0.28209479177387814
SH_ONE = 0.4886025119029199
SH_TWO = [
    1.0925484305920792,
    -1.0925484305920792,
    0.31539156525252005,
    -1.0925484305920792,
    0.5462742152960396,
]
SH_THREE = [
    -0.5900435899266435,
    2.890611442640554,
    -0.4570457994644658,
    0.3731763325901154,
    -0.4570457994644658,
    1.445305721320277,
    -0.5900435899266435,
]
F32 = jnp.float32
BF16 = jnp.bfloat16
MESH = pl.DeviceIdType.MESH
NEVER = -1e30


def learning_rates():
    return np.concatenate(
        [
            np.full(6, 0.016),
            np.full(3, 0.005),
            np.full(4, 0.001),
            np.full(1, 0.05),
            np.full(3, 0.0025),
            np.full(45, 0.000125),
        ]
    ).astype(np.float32)


def kernel_taps():
    raw_taps = [math.exp(-(offset * offset) / 4.5) for offset in range(-5, 6)]
    tap_total = sum(raw_taps)
    return [raw_tap / tap_total for raw_tap in raw_taps]


def up8(value):
    return (value + 7) // 8 * 8


def smoothing_tables(rows, cols, channels):
    taps = kernel_taps()
    in_rows, mid_rows = up8(rows + 2 * REACH), up8(rows + REACH)
    across = np.zeros((cols, cols), np.float32)
    for out in range(cols):
        for m in range(-HALO, HALO + 1):
            if 0 <= out + m < cols:
                across[out + m, out] = taps[m + HALO]
    first = np.zeros((channels * mid_rows, channels * in_rows), np.float32)
    second = np.zeros((channels * rows, channels * mid_rows), np.float32)
    for c in range(channels):
        for e in range(rows + REACH):
            for m in range(REACH + 1):
                first[c * mid_rows + e, c * in_rows + e + m] = taps[m]
        for i in range(rows):
            for m in range(REACH + 1):
                second[c * rows + i, c * mid_rows + i + m] = taps[m]
    return across, first, second


def power_table(tiles, cols):
    lane = np.arange(cols)
    local = lane % TILE + 0.5 - TILE / 2
    belongs = (lane[None, :] // TILE == np.arange(tiles)[:, None]).astype(np.float32)
    return np.concatenate([belongs, belongs * local, belongs * local * local]).astype(np.float32)


def harmonics(dir_x, dir_y, dir_z):
    sq_x, sq_y, sq_z = (dir_x * dir_x, dir_y * dir_y, dir_z * dir_z)
    return [
        SH_ZERO + 0.0 * dir_x,
        -SH_ONE * dir_y,
        SH_ONE * dir_z,
        -SH_ONE * dir_x,
        SH_TWO[0] * dir_x * dir_y,
        SH_TWO[1] * dir_y * dir_z,
        SH_TWO[2] * (2.0 * sq_z - sq_x - sq_y),
        SH_TWO[3] * dir_x * dir_z,
        SH_TWO[4] * (sq_x - sq_y),
        SH_THREE[0] * dir_y * (3.0 * sq_x - sq_y),
        SH_THREE[1] * dir_x * dir_y * dir_z,
        SH_THREE[2] * dir_y * (4.0 * sq_z - sq_x - sq_y),
        SH_THREE[3] * dir_z * (2.0 * sq_z - 3.0 * sq_x - 3.0 * sq_y),
        SH_THREE[4] * dir_x * (4.0 * sq_z - sq_x - sq_y),
        SH_THREE[5] * dir_z * (sq_x - sq_y),
        SH_THREE[6] * dir_x * (sq_x - 3.0 * sq_y),
    ]


def camera_basis(affine):
    a, b = affine[0:3], affine[3:6]
    n_x = a[1] * b[2] - a[2] * b[1]
    n_y = a[2] * b[0] - a[0] * b[2]
    n_z = a[0] * b[1] - a[1] * b[0]
    length = jnp.sqrt(n_x * n_x + n_y * n_y + n_z * n_z)
    return harmonics(n_x / length, n_y / length, n_z / length)


def shape_of(affine, logs, quats, logit):
    scales = [jnp.exp(value) for value in logs]
    quat_len = jnp.sqrt(
        quats[0] * quats[0] + quats[1] * quats[1] + quats[2] * quats[2] + quats[3] * quats[3]
    )
    r, i, j, k = [value / quat_len for value in quats]
    rotation = [
        [1.0 - 2.0 * (j * j + k * k), 2.0 * (i * j - r * k), 2.0 * (i * k + r * j)],
        [2.0 * (i * j + r * k), 1.0 - 2.0 * (i * i + k * k), 2.0 * (j * k - r * i)],
        [2.0 * (i * k - r * j), 2.0 * (j * k + r * i), 1.0 - 2.0 * (i * i + j * j)],
    ]
    m = [
        [
            (
                affine[3 * o] * rotation[0][c]
                + affine[3 * o + 1] * rotation[1][c]
                + affine[3 * o + 2] * rotation[2][c]
            )
            * scales[c]
            for c in range(3)
        ]
        for o in range(2)
    ]
    conic_a = m[0][0] * m[0][0] + m[0][1] * m[0][1] + m[0][2] * m[0][2] + 0.3
    conic_b = m[0][0] * m[1][0] + m[0][1] * m[1][1] + m[0][2] * m[1][2]
    conic_c = m[1][0] * m[1][0] + m[1][1] * m[1][1] + m[1][2] * m[1][2] + 0.3
    opacity = 1.0 / (1.0 + jnp.exp(-logit))
    return conic_a, conic_b, conic_c, opacity


def split3(value, axis=0):
    high = value.astype(BF16)
    rest = value - high.astype(F32)
    middle = rest.astype(BF16)
    low = (rest - middle.astype(F32)).astype(BF16)
    return high, middle, low


def exact_dot(table, value, dims):
    table = table.astype(BF16)
    total = None
    for part in split3(value):
        term = lax.dot_general(table, part, (dims, ((), ())), preferred_element_type=F32)
        total = term if total is None else total + term
    return total


def expand_dot(value, table):
    table = table.astype(BF16)
    total = None
    for part in split3(value):
        term = lax.dot_general(
            part, table, (((0,), (0,)), ((), ())), preferred_element_type=F32
        )
        total = term if total is None else total + term
    return total


NN = ((1,), (0,))
NT = ((1,), (1,))


def requests_of(messages, base, list_len, blocks):
    devices = messages.shape[0]
    block_iota = lax.broadcasted_iota(jnp.int32, (devices, blocks), 1).astype(F32) + base
    hit = jnp.zeros((devices, blocks), F32)
    for i in range(list_len):
        wanted = messages[:, 16 + i : 17 + i]
        hit = hit + jnp.where(wanted == block_iota, 1.0, 0.0)
    return hit


def tree_sum(vregs, lane_count):
    sub = lax.broadcasted_iota(jnp.int32, (8, lane_count), 0)

    def join(a, b, mask, shift):
        return jnp.where(mask, a, b) + pltpu.roll(jnp.where(mask, b, a), 8 - shift, 0)

    def half(offset):
        return ((sub + (8 - offset)) % 8) < 4

    def quarter(offset):
        return ((sub + (8 - offset)) % 4) < 2

    z1 = join(
        join(vregs[0], vregs[4], half(0), 4), join(vregs[2], vregs[6], half(2), 4), quarter(0), 2
    )
    z2 = join(
        join(vregs[1], vregs[5], half(1), 4), join(vregs[3], vregs[7], half(3), 4), quarter(1), 2
    )
    return join(z1, z2, (sub % 2) < 1, 1)


def step_kernel(
    geometry,
    camera_ref,
    list_ref,
    start_ref,
    end_ref,
    target_ref,
    gauss_hbm,
    across_ref,
    first_ref,
    second_ref,
    power_ref,
    incoming_ref,
    messages_ref,
    gauss_ref,
    msg_out,
    msg_in,
    geo_out,
    geo_in,
    tint_out,
    tint_in,
    grad_out,
    grad_in,
    halo_out,
    halo_in,
    thalo_out,
    thalo_in,
    coef,
    alpha_s,
    trans_s,
    moment_s,
    send_sem,
    recv_sem,
    halo_send,
    halo_recv,
    fetch_sem,
):
    views_n, bands_n, blocks, list_len, rows, cols, block_len = geometry
    devices = views_n * bands_n
    tiles = cols // TILE
    pairs = TILE_MOST * tiles
    window = TILE_MOST * block_len
    halves = block_len // 128
    view = lax.axis_index("view")
    band = lax.axis_index("band")
    me = view * bands_n + band
    base = (me * blocks).astype(F32)
    has_up = band > 0
    has_down = band < bands_n - 1

    def peer_of(d):
        return (lax.rem(view + d, views_n), lax.rem(band + d // views_n, bands_n))

    fetch = pltpu.make_async_copy(gauss_hbm, gauss_ref, fetch_sem.at[0])
    fetch.start()

    msg_out[...] = jnp.zeros_like(msg_out)
    msg_out[:, 0:9] = camera_ref[...]
    list_row = list_ref[0].astype(F32)
    msg_out[:, 16 : 16 + list_len] = list_row
    halo_in[...] = jnp.zeros_like(halo_in)
    thalo_in[...] = jnp.zeros_like(thalo_in)
    thalo_out[0] = target_ref[0, :, 0:REACH, :]
    thalo_out[1] = target_ref[0, :, rows - REACH : rows, :]
    barrier = pltpu.get_barrier_semaphore()

    def greet(d, carry):
        pl.semaphore_signal(barrier, inc=1, device_id=peer_of(d), device_id_type=MESH)
        return carry

    lax.fori_loop(1, devices, greet, 0)
    pl.semaphore_wait(barrier, devices - 1)

    def to_all(source_of, landing, phase):
        def send(d, carry):
            peer_view, peer_band = peer_of(d)
            peer = peer_view * bands_n + peer_band
            pltpu.make_async_remote_copy(
                src_ref=source_of(peer),
                dst_ref=landing.at[me],
                send_sem=send_sem.at[phase],
                recv_sem=recv_sem.at[phase],
                device_id=peer_of(d),
                device_id_type=MESH,
            ).start()
            return carry

        lax.fori_loop(1, devices, send, 0)

    def wait_all(landing, phase):
        every = landing.at[pl.ds(0, devices - 1)]
        pltpu.make_async_copy(every, every, recv_sem.at[phase]).wait()
        pltpu.make_async_copy(every, every, send_sem.at[phase]).wait()

    def edge_copy(source, landing, direction, phase):
        step = -1 if direction == 0 else 1
        return pltpu.make_async_remote_copy(
            src_ref=source.at[direction],
            dst_ref=landing.at[1 - direction],
            send_sem=halo_send.at[phase, direction],
            recv_sem=halo_recv.at[phase, 1 - direction],
            device_id=(view, band + step),
            device_id_type=MESH,
        )

    def edges_start(source, landing, phase):
        @pl.when(has_up)
        def _():
            edge_copy(source, landing, 0, phase).start()

        @pl.when(has_down)
        def _():
            edge_copy(source, landing, 1, phase).start()

    def edges_wait(source, landing, phase):
        @pl.when(has_up)
        def _():
            up = edge_copy(source, landing, 0, phase)
            up.wait_send()
            pltpu.make_async_copy(
                landing.at[0], landing.at[0], halo_recv.at[phase, 0]
            ).wait()

        @pl.when(has_down)
        def _():
            down = edge_copy(source, landing, 1, phase)
            down.wait_send()
            pltpu.make_async_copy(
                landing.at[1], landing.at[1], halo_recv.at[phase, 1]
            ).wait()

    to_all(lambda peer: msg_out, msg_in, 0)
    edges_start(thalo_out, thalo_in, 0)
    msg_in[me] = msg_out[...]

    owner_low = lax.broadcasted_iota(jnp.int32, (devices, list_len), 0).astype(F32) * blocks
    owner_hot = jnp.where((list_row >= owner_low) & (list_row < owner_low + blocks), 1.0, 0.0)
    pair_row = lax.broadcasted_iota(jnp.int32, (pairs, tiles), 0)
    on_tile = pair_row % tiles == lax.broadcasted_iota(jnp.int32, (pairs, tiles), 1)

    def upright(row):
        return jnp.sum(jnp.where(on_tile, row.astype(F32), 0.0), axis=1, keepdims=True)

    later = (lax.broadcasted_iota(jnp.int32, (pairs, 1), 0) // tiles).astype(F32)
    spot = upright(start_ref[0]) + later
    position = lax.broadcasted_iota(jnp.int32, (pairs, list_len), 1).astype(F32)
    place = jnp.where((position == spot) & (spot < upright(end_ref[0])), 1.0, 0.0)
    live_pair = jnp.max(place, axis=1, keepdims=True)
    pick_owner = lax.dot_general(
        place.astype(BF16), owner_hot.astype(BF16), (NT, ((), ())), preferred_element_type=F32
    )
    put_owner = lax.dot_general(
        owner_hot.astype(BF16), place.astype(BF16), (NT, ((), ())), preferred_element_type=F32
    )
    live = jnp.concatenate(
        [
            jnp.broadcast_to(live_pair[k * tiles : (k + 1) * tiles], (tiles, block_len))
            for k in range(TILE_MOST)
        ],
        axis=1,
    )

    wait_all(msg_in, 0)
    fetch.wait()

    asked = msg_in[...].reshape(devices, 128)
    messages_ref[...] = asked
    hot = requests_of(asked, base, list_len, blocks)
    missing = 1.0 - jnp.max(hot, axis=1, keepdims=True)
    cam = [asked[:, c : c + 1] for c in range(9)]

    def picked(component):
        return exact_dot(hot, gauss_ref[component], NN)

    centre = [picked(c) + cam[8] * picked(3 + c) for c in range(3)]
    records = [
        cam[0] * centre[0] + cam[1] * centre[1] + cam[2] * centre[2] + cam[6],
        cam[3] * centre[0] + cam[4] * centre[1] + cam[5] * centre[2] + cam[7],
    ]
    quats = [picked(9 + c) for c in range(4)]
    quats[0] = quats[0] + missing
    conic_a, conic_b, conic_c, opacity = shape_of(
        cam[0:6], [picked(6 + c) for c in range(3)], quats, picked(13)
    )
    records += [conic_a, conic_b, conic_c, opacity]
    for p in range(GEO_REC):
        for h in range(halves):
            geo_out[:, p * halves + h, :] = records[p][:, h * 128 : (h + 1) * 128]
    to_all(lambda peer: geo_out.at[peer], geo_in, 1)
    geo_in[me] = geo_out[me]
    basis = camera_basis(cam)
    basis = [jnp.where(missing > 0.5, 0.0, value) for value in basis]
    for ch in range(3):
        colour = 0.5
        for q in range(16):
            colour = colour + basis[q] * picked(14 + 3 * q + ch)
        for h in range(halves):
            tint_out[:, ch * halves + h, :] = colour[:, h * 128 : (h + 1) * 128]
    to_all(lambda peer: tint_out.at[peer], tint_in, 2)
    tint_in[me] = tint_out[me]
    wait_all(geo_in, 1)

    def gathered(landed, p):
        parts = []
        for h in range(halves):
            parts.append(exact_dot(pick_owner, landed[:, p * halves + h, :], NN))
        whole = jnp.concatenate(parts, axis=1)
        return jnp.concatenate(
            [whole[k * tiles : (k + 1) * tiles] for k in range(TILE_MOST)], axis=1
        )

    dead = 1.0 - live
    tile_row = lax.broadcasted_iota(jnp.int32, (tiles, window), 0).astype(F32)
    u_rel = gathered(geo_in, 0) - (tile_row * TILE + 0.5 * TILE)
    w_rel = gathered(geo_in, 1) - ((band * rows).astype(F32) + 0.5 * TILE)
    c_a = gathered(geo_in, 2) + dead
    c_b = gathered(geo_in, 3)
    c_c = gathered(geo_in, 4) + dead
    opac = gathered(geo_in, 5) + dead
    inv_det = 1.0 / (c_a * c_c - c_b * c_b)
    coef_a = -0.5 * c_c * inv_det
    coef_b = c_b * inv_det
    coef_c = -0.5 * c_a * inv_det
    keep = live > 0.5

    def masked(value, other=0.0):
        return jnp.where(keep, value, other)

    flat = LOG2_E * (
        coef_a * u_rel * u_rel + coef_b * u_rel * w_rel + coef_c * w_rel * w_rel
    ) + LOG2_E * jnp.log(opac)
    power = power_ref[...]
    coef[0] = expand_dot(
        jnp.concatenate(
            [
                masked(flat, NEVER),
                masked(LOG2_E * (-2.0 * coef_a * u_rel - coef_b * w_rel)),
                masked(LOG2_E * coef_a),
            ],
            axis=0,
        ),
        power,
    )
    coef[1] = expand_dot(
        jnp.concatenate(
            [
                masked(LOG2_E * (-coef_b * u_rel - 2.0 * coef_c * w_rel)),
                masked(LOG2_E * coef_b),
            ],
            axis=0,
        ),
        power[0 : 2 * tiles],
    )
    coef[2] = expand_dot(masked(LOG2_E * coef_c), power[0:tiles])
    wait_all(tint_in, 2)
    for ch in range(3):
        coef[3 + ch] = expand_dot(masked(gathered(tint_in, ch)), power[0:tiles])

    sub8 = lax.broadcasted_iota(jnp.int32, (8, cols), 0).astype(F32)
    parts_n = rows // 8
    row_local = [sub8 + (8.0 * part + 0.5 - 0.5 * TILE) for part in range(parts_n)]

    def spread_row(kind, j):
        return coef[kind, pl.ds(j, 8, stride=0), :]

    def blend(group, carry):
        trans, image = carry
        trans, image = list(trans), list(image)
        for k in range(8):
            j = group * 8 + k
            q0, q1, q2 = spread_row(0, j), spread_row(1, j), spread_row(2, j)
            tint = [spread_row(3 + ch, j) for ch in range(3)]
            for part in range(parts_n):
                r = row_local[part]
                alpha = jnp.exp2(q0 + r * (q1 + r * q2))
                weight = alpha * trans[part]
                alpha_s[j, part] = alpha
                trans_s[j, part] = trans[part]
                trans[part] = trans[part] - weight
                for ch in range(3):
                    at = ch * parts_n + part
                    image[at] = image[at] + weight * tint[ch]
        return tuple(trans), tuple(image)

    zero = jnp.zeros((8, cols), F32)
    _, image = lax.fori_loop(
        0,
        window // 8,
        blend,
        (tuple([zero + 1.0] * parts_n), tuple([zero] * (3 * parts_n))),
    )
    pred = [
        jnp.concatenate([image[ch * parts_n + part] for part in range(parts_n)], axis=0)
        for ch in range(3)
    ]
    for ch in range(3):
        halo_out[0, ch] = pred[ch][0:REACH]
        halo_out[1, ch] = pred[ch][rows - REACH : rows]
    edges_start(halo_out, halo_in, 1)
    edges_wait(thalo_out, thalo_in, 0)
    edges_wait(halo_out, halo_in, 1)

    in_rows, mid_rows = up8(rows + 2 * REACH), up8(rows + REACH)
    fill = jnp.zeros((in_rows - rows - 2 * REACH, cols), F32)
    mine = target_ref[0]
    ext_x = jnp.concatenate(
        [v for ch in range(3) for v in (halo_in[0, ch], pred[ch], halo_in[1, ch], fill)], axis=0
    )
    ext_y = jnp.concatenate(
        [v for ch in range(3) for v in (thalo_in[0, ch], mine[ch], thalo_in[1, ch], fill)], axis=0
    )
    fields = jnp.concatenate(
        [ext_x, ext_y, ext_x * ext_x, ext_y * ext_y, ext_x * ext_y], axis=1
    )
    down = jnp.dot(first_ref[...], fields, precision=HIGHEST_MODE, preferred_element_type=F32)
    stacked = jnp.concatenate([down[:, f * cols : (f + 1) * cols] for f in range(5)], axis=0)
    smoothed = jnp.dot(
        stacked, across_ref[...], precision=HIGHEST_MODE, preferred_element_type=F32
    )
    high = 3 * mid_rows
    mean_x, mean_y, square_x, square_y, cross = [
        smoothed[f * high : (f + 1) * high] for f in range(5)
    ]
    n_mean = 2.0 * mean_x * mean_y + STAB_MEAN
    n_var = 2.0 * (cross - mean_x * mean_y) + STAB_VAR
    d_mean = mean_x * mean_x + mean_y * mean_y + STAB_MEAN
    d_var = (square_x - mean_x * mean_x) + (square_y - mean_y * mean_y) + STAB_VAR
    inv_mean = 1.0 / d_mean
    inv_var = 1.0 / d_var
    inverse = inv_mean * inv_var
    ssim = n_mean * n_var * inverse
    ext_row = lax.broadcasted_iota(jnp.int32, (high, cols), 0) % mid_rows
    image_row = ext_row + (band * rows - HALO)
    inside = (image_row >= 0) & (image_row < bands_n * rows) & (ext_row < rows + REACH)
    scale = -SSIM_WEIGHT / 3.0
    part_mean = 2.0 * mean_y * (n_var - n_mean) * inverse - 2.0 * mean_x * ssim * (
        inv_mean - inv_var
    )
    adjoint = jnp.concatenate(
        [
            jnp.where(inside, scale * part_mean, 0.0),
            jnp.where(inside, -scale * ssim * inv_var, 0.0),
            jnp.where(inside, (2.0 * scale) * n_mean * inverse, 0.0),
        ],
        axis=1,
    )
    down2 = jnp.dot(second_ref[...], adjoint, precision=HIGHEST_MODE, preferred_element_type=F32)
    stacked2 = jnp.concatenate([down2[:, f * cols : (f + 1) * cols] for f in range(3)], axis=0)
    spread = jnp.dot(
        stacked2, across_ref[...], precision=HIGHEST_MODE, preferred_element_type=F32
    )
    deep = 3 * rows
    pred_all = jnp.concatenate(pred, axis=0)
    mine_all = jnp.concatenate([mine[ch] for ch in range(3)], axis=0)
    error = pred_all - mine_all
    sign = jnp.where(error > 0.0, 1.0, jnp.where(error < 0.0, -1.0, 0.0))
    grad_pred = (
        ABS_WEIGHT / 3.0 * sign
        + spread[0:deep]
        + 2.0 * pred_all * spread[deep : 2 * deep]
        + mine_all * spread[2 * deep : 3 * deep]
    )
    own = (ext_row >= HALO) & (ext_row < HALO + rows)
    loss = jnp.sum(ABS_WEIGHT / 3.0 * jnp.abs(error), keepdims=True) + jnp.sum(
        jnp.where(own, SSIM_WEIGHT / 3.0 * (1.0 - ssim), 0.0), keepdims=True
    )

    pull = [
        [grad_pred[ch * rows + 8 * part : ch * rows + 8 * part + 8] for part in range(parts_n)]
        for ch in range(3)
    ]

    def unblend(step, behind):
        group = window // 8 - 1 - step
        behind = list(behind)
        sums = [[None] * 8 for _ in range(6)]
        for k in reversed(range(8)):
            j = group * 8 + k
            tint = [spread_row(3 + ch, j) for ch in range(3)]
            totals = [None] * 6
            for part in range(parts_n):
                alpha = alpha_s[j, part]
                trans = trans_s[j, part]
                shade = (
                    tint[0] * pull[0][part] + tint[1] * pull[1][part] + tint[2] * pull[2][part]
                )
                gap = shade - behind[part]
                behind[part] = behind[part] + alpha * gap
                weight = alpha * trans
                lean = weight * gap
                lean_r = lean * row_local[part]
                terms = [lean, lean_r, lean_r * row_local[part]]
                terms += [weight * pull[ch][part] for ch in range(3)]
                totals = [
                    term if total is None else total + term for term, total in zip(terms, totals)
                ]
            for kind in range(6):
                sums[kind][k] = totals[kind]
        at = pl.multiple_of(group * 8, 8)
        for kind in range(6):
            moment_s[kind, pl.ds(at, 8), :] = tree_sum(sums[kind], cols)
        return tuple(behind)

    lax.fori_loop(0, window // 8, unblend, tuple([zero] * parts_n))

    by_x = exact_dot(power, moment_s[0], NT)
    m_00, m_10, m_20 = by_x[0:tiles], by_x[tiles : 2 * tiles], by_x[2 * tiles : 3 * tiles]
    by_xr = exact_dot(power[0 : 2 * tiles], moment_s[1], NT)
    m_01, m_11 = by_xr[0:tiles], by_xr[tiles : 2 * tiles]
    m_02 = exact_dot(power[0:tiles], moment_s[2], NT)
    s_x = m_10 - u_rel * m_00
    s_y = m_01 - w_rel * m_00
    s_xx = m_20 - 2.0 * u_rel * m_10 + u_rel * u_rel * m_00
    s_xy = m_11 - u_rel * m_01 - w_rel * m_10 + u_rel * w_rel * m_00
    s_yy = m_02 - 2.0 * w_rel * m_01 + w_rel * w_rel * m_00
    by_det = -(coef_a * s_xx + coef_b * s_xy + coef_c * s_yy) * inv_det
    derivs = [
        -(2.0 * coef_a * s_x + coef_b * s_y),
        -(2.0 * coef_c * s_y + coef_b * s_x),
        -0.5 * inv_det * s_yy + by_det * c_c,
        inv_det * s_xy - 2.0 * c_b * by_det,
        -0.5 * inv_det * s_xx + by_det * c_a,
        m_00 / opac,
    ] + [exact_dot(power[0:tiles], moment_s[3 + ch], NT) for ch in range(3)]
    for p in range(ROW_REC):
        split_pairs = jnp.concatenate(
            [derivs[p][:, k * block_len : (k + 1) * block_len] for k in range(TILE_MOST)], axis=0
        )
        routed = exact_dot(put_owner, split_pairs, NN)
        for h in range(halves):
            grad_out[:, p * halves + h, :] = routed[:, h * 128 : (h + 1) * 128]
    grad_out[:, ROW_REC * halves, :] = jnp.broadcast_to(loss, (devices, 128))
    to_all(lambda peer: grad_out.at[peer], grad_in, 3)
    grad_in[me] = grad_out[me]
    wait_all(grad_in, 3)
    incoming_ref[...] = grad_in[...]


def adam_kernel(
    geometry,
    messages_ref,
    incoming_ref,
    rates_ref,
    gauss_ref,
    one_ref,
    two_ref,
    out_gauss,
    out_one,
    out_two,
    out_loss,
    out_grad_hbm,
    out_grad,
    one_v,
    two_v,
    gauss_v,
    read_sem,
    write_sem,
):
    fetch_one = pltpu.make_async_copy(one_ref, one_v, read_sem.at[0])
    fetch_two = pltpu.make_async_copy(two_ref, two_v, read_sem.at[1])
    fetch_one.start()
    fetch_two.start()
    views_n, bands_n, blocks, list_len, rows, cols, block_len = geometry
    devices = views_n * bands_n
    halves = block_len // 128
    me = lax.axis_index("view") * bands_n + lax.axis_index("band")
    base = (me * blocks).astype(F32)
    asked = messages_ref[...]
    hot = requests_of(asked, base, list_len, blocks)
    missing = 1.0 - jnp.max(hot, axis=1, keepdims=True)
    cam = [asked[:, c : c + 1] for c in range(9)]

    def picked(component):
        return exact_dot(hot, gauss_ref[component], NN)

    def arrived(p):
        return jnp.concatenate(
            [incoming_ref[:, p * halves + h, :] for h in range(halves)], axis=1
        )

    d_u, d_w = arrived(0), arrived(1)
    columns = []
    along = [cam[c] * d_u + cam[3 + c] * d_w for c in range(3)]
    columns += along + [cam[8] * value for value in along]
    quats = [picked(9 + c) for c in range(4)]
    quats[0] = quats[0] + missing
    logs = [picked(6 + c) for c in range(3)]
    _, pullback = jax.vjp(
        lambda a, b, c: shape_of(cam[0:6], a, b, c), logs, quats, picked(13)
    )
    d_logs, d_quats, d_logit = pullback(tuple(arrived(2 + p) for p in range(4)))
    columns += list(d_logs) + list(d_quats) + [d_logit]
    turned = jnp.transpose(jnp.concatenate([asked] * 3, axis=0))
    hot_t = jnp.transpose(hot)
    for c in range(14):
        out_grad[c] = exact_dot(hot_t, columns[c], NN)
    basis = camera_basis([turned[c : c + 1, :] for c in range(6)])
    channel = lax.broadcasted_iota(jnp.int32, (3, 3 * devices), 1) // devices
    own_channel = channel == lax.broadcasted_iota(jnp.int32, (3, 3 * devices), 0)
    fan = jnp.concatenate([jnp.where(own_channel, value, 0.0) for value in basis], axis=0)
    hot_3 = jnp.transpose(jnp.concatenate([hot] * 3, axis=0))
    shades = fan.shape[0]
    routed = jnp.concatenate([hot_3 * fan[r : r + 1, :] for r in range(shades)], axis=0)
    tinted = jnp.concatenate([arrived(6 + ch) for ch in range(3)], axis=0)
    colour = jnp.dot(routed, tinted, precision=HIGHEST_MODE, preferred_element_type=F32)
    for r in range(shades):
        out_grad[14 + r] = colour[r * blocks : (r + 1) * blocks]
    losses = incoming_ref[:, ROW_REC * halves, :]
    out_loss[...] = jnp.sum(losses, axis=0, keepdims=True)[:, 0:1] * (
        1.0 / (devices * rows * cols)
    )
    fetch_one.wait()
    fetch_two.wait()
    comps = gauss_ref.shape[0]
    pieces = []
    for piece in range(PIECES):
        low, high = piece * comps // PIECES, (piece + 1) * comps // PIECES

        def update(c, carry):
            gradient = out_grad[c]
            new_one = 0.9 * one_v[c] + 0.1 * gradient
            new_two = 0.999 * two_v[c] + 0.001 * gradient * gradient
            one_v[c] = new_one
            two_v[c] = new_two
            bottom = jnp.sqrt(new_two * (1.0 / BIAS_SECOND)) + 1e-08
            gauss_v[c] = gauss_ref[c] - rates_ref[c] * new_one / bottom
            return carry

        lax.fori_loop(low, high, update, 0, unroll=2)
        part = pl.ds(low, high - low)
        for source, landing, sem in (
            (one_v, out_one, 0),
            (two_v, out_two, 1),
            (gauss_v, out_gauss, 2),
            (out_grad, out_grad_hbm, 3),
        ):
            copy = pltpu.make_async_copy(
                source.at[part], landing.at[part], write_sem.at[sem, piece]
            )
            copy.start()
            pieces.append(copy)
    for copy in pieces:
        copy.wait()


def per_device(
    gaussians,
    first_moment,
    second_moment,
    camera,
    target,
    block_list,
    block_count,
    tile_start,
    tile_end,
):
    views_n = lax.axis_size("view")
    bands_n = lax.axis_size("band")
    devices = views_n * bands_n
    blocks, comps, block_len = gaussians.shape
    list_len = block_list.shape[2]
    rows, cols = target.shape[2:]
    tiles = cols // TILE
    halves = block_len // 128
    geometry = (views_n, bands_n, blocks, list_len, rows, cols, block_len)

    across, first, second = smoothing_tables(rows, cols, 3)
    power = power_table(tiles, cols)
    vmem = pl.BlockSpec(memory_space=pltpu.VMEM)
    hbm = pl.BlockSpec(memory_space=pl.ANY)

    def by_comp(array):
        return jnp.transpose(array, (1, 0, 2))

    rec_rows = ROW_REC * halves
    window = TILE_MOST * block_len
    incoming, messages = pl.pallas_call(
        functools.partial(step_kernel, geometry),
        out_shape=(
            jax.ShapeDtypeStruct((devices, rec_rows + 1, 128), F32),
            jax.ShapeDtypeStruct((devices, 128), F32),
        ),
        in_specs=[vmem] * 5 + [hbm] + [vmem] * 4,
        out_specs=(vmem, vmem),
        scratch_shapes=[
            pltpu.VMEM((comps, blocks, block_len), F32),
            pltpu.VMEM((1, 128), F32),
            pltpu.VMEM((devices, 1, 128), F32),
            pltpu.VMEM((devices, GEO_REC * halves, 128), F32),
            pltpu.VMEM((devices, GEO_REC * halves, 128), F32),
            pltpu.VMEM((devices, rec_rows - GEO_REC * halves, 128), F32),
            pltpu.VMEM((devices, rec_rows - GEO_REC * halves, 128), F32),
            pltpu.VMEM((devices, rec_rows + 1, 128), F32),
            pltpu.VMEM((devices, rec_rows + 1, 128), F32),
            pltpu.VMEM((2, 3, REACH, cols), F32),
            pltpu.VMEM((2, 3, REACH, cols), F32),
            pltpu.VMEM((2, 3, REACH, cols), F32),
            pltpu.VMEM((2, 3, REACH, cols), F32),
            pltpu.VMEM((6, window, cols), F32),
            pltpu.VMEM((window, rows // 8, 8, cols), F32),
            pltpu.VMEM((window, rows // 8, 8, cols), F32),
            pltpu.VMEM((6, window, cols), F32),
            pltpu.SemaphoreType.DMA((4,)),
            pltpu.SemaphoreType.DMA((4,)),
            pltpu.SemaphoreType.DMA((2, 2)),
            pltpu.SemaphoreType.DMA((2, 2)),
            pltpu.SemaphoreType.DMA((1,)),
        ],
        compiler_params=pltpu.CompilerParams(collective_id=0, has_side_effects=True),
        name="render_step",
    )(
        camera,
        block_list,
        tile_start,
        tile_end,
        target,
        by_comp(gaussians),
        across,
        first,
        second,
        power,
    )

    rates = learning_rates() / BIAS_FIRST
    shape = jax.ShapeDtypeStruct((comps, blocks, block_len), F32)
    new_params, new_one, new_two, mean_loss, gradient = pl.pallas_call(
        functools.partial(adam_kernel, geometry),
        out_shape=(shape, shape, shape, jax.ShapeDtypeStruct((1, 1), F32), shape),
        in_specs=[vmem, vmem, pl.BlockSpec(memory_space=pltpu.SMEM), vmem, hbm, hbm],
        out_specs=(hbm, hbm, hbm, vmem, hbm),
        scratch_shapes=[pltpu.VMEM((comps, blocks, block_len), F32)] * 4
        + [pltpu.SemaphoreType.DMA((2,)), pltpu.SemaphoreType.DMA((4, PIECES))],
        name="adam_step",
    )(
        messages,
        incoming,
        rates,
        by_comp(gaussians),
        by_comp(first_moment),
        by_comp(second_moment),
    )
    return (
        by_comp(new_params),
        by_comp(new_one),
        by_comp(new_two),
        mean_loss.reshape(()),
        by_comp(gradient),
    )


def solution(mesh):
    return jax.shard_map(
        per_device,
        mesh=mesh,
        in_specs=(
            P(("view", "band"), None, None),
            P(("view", "band"), None, None),
            P(("view", "band"), None, None),
            P("view", None),
            P("view", None, "band", None),
            P("view", "band", None),
            P("view", "band"),
            P("view", "band", None),
            P("view", "band", None),
        ),
        out_specs=(
            P(("view", "band"), None, None),
            P(("view", "band"), None, None),
            P(("view", "band"), None, None),
            P(),
            P(("view", "band"), None, None),
        ),
        check_vma=False,
    )
```

profile of v0, /device:TPU:0, one launch (start us, length us, event | category | flops | bytes accessed | tf_op | source)
XLA Modules:
  0.0 50.4 jit_solution(619486827050458678)
XLA Ops:
  0.6 43.9 %render_step.1 = (f32[32,19,128]{2,1,0:T(8,128)}, f32[32,128]{1,0:T(8,128)}) custom-call(f32[1,9]{1,0:T(1,128)} %camera_ref.1, s32[1,1,16]{2,1,0:T(1,128)} %list_ref.1, s32[1,1,8]{2,1,0:T(1,128)} %start_ref.1, s32[1,1,8]{2,1,0:T(1,128)} %end_ref.1, f32[1,3,16,128]{3,2,1,0:T(8,128)} %target_ref.1, f32[62,16,256]{2,1,0:T(8,128)} %bitcast.8, ...), custom_call_target="tpu_custom_call" | custom-call | tf_op jit(solution)/shard_map/render_step/pallas_call | solution.py:802
  44.6 5.8 %adam_step.1 = (f32[62,16,256]{2,1,0:T(8,128)}, f32[62,16,256]{2,1,0:T(8,128)}, f32[62,16,256]{2,1,0:T(8,128)}, f32[1,1]{1,0:T(1,128)}, f32[62,16,256]{2,1,0:T(8,128)}) custom-call(f32[32,128]{1,0:T(8,128)} %get-tuple-element.12.messages_ref, f32[32,19,128]{2,1,0:T(8,128)} %get-tuple-element.13.incoming_ref, f32[62]{0:T(128)} %constant.14.clone.rates_ref, ...), custom_call_target="tpu_custom_call" | custom-call | tf_op jit(solution)/shard_map/adam_step/pallas_call | solution.py:851
where the time goes:
time: 50.6 us; the launch traced here: 50.4 us
  Pallas kernels  49.8 us (98%)
  between operations  0.64 us (1%)
    pallas_call x1, Pallas kernels, per_device(): pl.pallas_call(functools.partial(step_kernel, geometry), out_shape=(jax.S...  43.9 us
    pallas_call x1, Pallas kernels, per_device(): pl.pallas_call(functools.partial(adam_kernel, geometry), out_shape=(shape...  5.83 us

commit v1 on v0

v1 whole, which is shorter than its diff:
```python
import functools
import math

import jax
import jax.numpy as jnp
import numpy as np
from jax import lax
from jax.experimental import pallas as pl
from jax.experimental.pallas import tpu as pltpu
from jax.sharding import PartitionSpec as P

TILE = 16
TILE_MOST = 2
HALO = 5
REACH = 2 * HALO
GEO_REC = 6
PIECES = 4

HIGHEST_MODE = lax.Precision.HIGHEST
SSIM_WEIGHT = 0.2
ABS_WEIGHT = 0.8
STAB_MEAN = 0.0001
STAB_VAR = 0.0009
BIAS_FIRST = 1.0 - math.exp(100.0 * math.log(0.9))
BIAS_SECOND = 1.0 - math.exp(100.0 * math.log(0.999))
LOG2_E = math.log2(math.e)
SH_ZERO = 0.28209479177387814
SH_ONE = 0.4886025119029199
SH_TWO = [
    1.0925484305920792,
    -1.0925484305920792,
    0.31539156525252005,
    -1.0925484305920792,
    0.5462742152960396,
]
SH_THREE = [
    -0.5900435899266435,
    2.890611442640554,
    -0.4570457994644658,
    0.3731763325901154,
    -0.4570457994644658,
    1.445305721320277,
    -0.5900435899266435,
]
F32 = jnp.float32
BF16 = jnp.bfloat16
MESH = pl.DeviceIdType.MESH
NEVER = -1e30


RATES = ((6, 0.016), (9, 0.005), (13, 0.001), (14, 0.05), (17, 0.0025), (62, 0.000125))


def learning_rate(component):
    rate = RATES[-1][1] / BIAS_FIRST
    for end, value in reversed(RATES[:-1]):
        rate = jnp.where(component < end, value / BIAS_FIRST, rate)
    return rate


def kernel_taps():
    raw_taps = [math.exp(-(offset * offset) / 4.5) for offset in range(-5, 6)]
    tap_total = sum(raw_taps)
    return [raw_tap / tap_total for raw_tap in raw_taps]


def up8(value):
    return (value + 7) // 8 * 8


def smoothing_tables(rows, cols, channels):
    taps = kernel_taps()
    in_rows, mid_rows = up8(rows + 2 * REACH), up8(rows + REACH)
    across = np.zeros((cols, cols), np.float32)
    for out in range(cols):
        for m in range(-HALO, HALO + 1):
            if 0 <= out + m < cols:
                across[out + m, out] = taps[m + HALO]
    first = np.zeros((channels * mid_rows, channels * in_rows), np.float32)
    second = np.zeros((channels * rows, channels * mid_rows), np.float32)
    for c in range(channels):
        for e in range(rows + REACH):
            for m in range(REACH + 1):
                first[c * mid_rows + e, c * in_rows + e + m] = taps[m]
        for i in range(rows):
            for m in range(REACH + 1):
                second[c * rows + i, c * mid_rows + i + m] = taps[m]
    return across, first, second


def power_table(tiles, cols):
    lane = np.arange(cols)
    local = lane % TILE + 0.5 - TILE / 2
    belongs = (lane[None, :] // TILE == np.arange(tiles)[:, None]).astype(np.float32)
    return np.concatenate([belongs, belongs * local, belongs * local * local]).astype(np.float32)


def harmonics(dir_x, dir_y, dir_z):
    sq_x, sq_y, sq_z = (dir_x * dir_x, dir_y * dir_y, dir_z * dir_z)
    return [
        SH_ZERO + 0.0 * dir_x,
        -SH_ONE * dir_y,
        SH_ONE * dir_z,
        -SH_ONE * dir_x,
        SH_TWO[0] * dir_x * dir_y,
        SH_TWO[1] * dir_y * dir_z,
        SH_TWO[2] * (2.0 * sq_z - sq_x - sq_y),
        SH_TWO[3] * dir_x * dir_z,
        SH_TWO[4] * (sq_x - sq_y),
        SH_THREE[0] * dir_y * (3.0 * sq_x - sq_y),
        SH_THREE[1] * dir_x * dir_y * dir_z,
        SH_THREE[2] * dir_y * (4.0 * sq_z - sq_x - sq_y),
        SH_THREE[3] * dir_z * (2.0 * sq_z - 3.0 * sq_x - 3.0 * sq_y),
        SH_THREE[4] * dir_x * (4.0 * sq_z - sq_x - sq_y),
        SH_THREE[5] * dir_z * (sq_x - sq_y),
        SH_THREE[6] * dir_x * (sq_x - 3.0 * sq_y),
    ]


def camera_basis(affine):
    a, b = affine[0:3], affine[3:6]
    n_x = a[1] * b[2] - a[2] * b[1]
    n_y = a[2] * b[0] - a[0] * b[2]
    n_z = a[0] * b[1] - a[1] * b[0]
    length = jnp.sqrt(n_x * n_x + n_y * n_y + n_z * n_z)
    return harmonics(n_x / length, n_y / length, n_z / length)


def split3(value, axis=0):
    high = value.astype(BF16)
    rest = value - high.astype(F32)
    middle = rest.astype(BF16)
    low = (rest - middle.astype(F32)).astype(BF16)
    return high, middle, low


NN = ((1,), (0,))
NT = ((1,), (1,))
TN = ((0,), (0,))


def mx(a, b, dims=NN):
    return lax.dot_general(a, b, (dims, ((), ())), preferred_element_type=F32)


def split2(value):
    high = value.astype(BF16)
    return high, (value - high.astype(F32)).astype(BF16)


def stack3(value):
    return jnp.concatenate(split3(value), axis=0)


def stack2(value):
    return jnp.concatenate(split2(value), axis=0)


def exact_dot(table, value, dims):
    table = table.astype(BF16)
    total = None
    for part in split3(value):
        term = mx(table, part, dims)
        total = term if total is None else total + term
    return total


def tree_sum(vregs, lane_count):
    sub = lax.broadcasted_iota(jnp.int32, (8, lane_count), 0)

    def join(a, b, mask, shift):
        return jnp.where(mask, a, b) + pltpu.roll(jnp.where(mask, b, a), 8 - shift, 0)

    def half(offset):
        return ((sub + (8 - offset)) % 8) < 4

    def quarter(offset):
        return ((sub + (8 - offset)) % 4) < 2

    z1 = join(
        join(vregs[0], vregs[4], half(0), 4), join(vregs[2], vregs[6], half(2), 4), quarter(0), 2
    )
    z2 = join(
        join(vregs[1], vregs[5], half(1), 4), join(vregs[3], vregs[7], half(3), 4), quarter(1), 2
    )
    return join(z1, z2, (sub % 2) < 1, 1)


def block_shape(logs, quats, logit):
    squares = [jnp.exp(value) for value in logs]
    squares = [value * value for value in squares]
    quat_len = jnp.sqrt(
        quats[0] * quats[0] + quats[1] * quats[1] + quats[2] * quats[2] + quats[3] * quats[3]
    )
    r, i, j, k = [value / quat_len for value in quats]
    rotation = [
        [1.0 - 2.0 * (j * j + k * k), 2.0 * (i * j - r * k), 2.0 * (i * k + r * j)],
        [2.0 * (i * j + r * k), 1.0 - 2.0 * (i * i + k * k), 2.0 * (j * k - r * i)],
        [2.0 * (i * k - r * j), 2.0 * (j * k + r * i), 1.0 - 2.0 * (i * i + j * j)],
    ]
    spread = [[rotation[a][c] * squares[c] for c in range(3)] for a in range(3)]

    def moment(a, b):
        return (
            spread[a][0] * rotation[b][0]
            + spread[a][1] * rotation[b][1]
            + spread[a][2] * rotation[b][2]
        )

    pairs = ((0, 0), (1, 1), (2, 2), (0, 1), (0, 2), (1, 2))
    return [moment(a, b) for a, b in pairs], 1.0 / (1.0 + jnp.exp(-logit))


def view_terms(cam):
    a, b, time = cam[0:3], cam[3:6], cam[8]
    terms = a + [time * value for value in a] + b + [time * value for value in b]
    crossed = ((0, 1), (0, 2), (1, 2))
    terms += [a[c] * a[c] for c in range(3)] + [2.0 * a[c] * a[d] for c, d in crossed]
    terms += [a[c] * b[c] for c in range(3)] + [a[c] * b[d] + a[d] * b[c] for c, d in crossed]
    terms += [b[c] * b[c] for c in range(3)] + [2.0 * b[c] * b[d] for c, d in crossed]
    return terms + [cam[6], cam[7]] + camera_basis(cam[0:6])


TERM_ROWS = 6
SHIFT_AT = 30
BASIS_AT = 32
BASIS = 16
TERMS = 48
GEO_COMPS = 13


def step_kernel(
    geometry,
    camera_hbm,
    list_hbm,
    start_hbm,
    end_hbm,
    target_hbm,
    gauss_hbm,
    one_hbm,
    two_hbm,
    across_hbm,
    first_hbm,
    second_hbm,
    power_hbm,
    quad_hbm,
    tone_hbm,
    grad_ref,
    gauss_ref,
    one_ref,
    two_ref,
    loss_ref,
    camera_s,
    list_s,
    start_s,
    end_s,
    target_ref,
    across_ref,
    first_ref,
    second_ref,
    power_ref,
    quad_ref,
    tone_ref,
    msg_out,
    msg_in,
    hot_map,
    wide_map,
    geo_tab,
    tint_tab,
    tint_back,
    line_back,
    shape_back,
    geo_out,
    geo_in,
    tint_out,
    tint_in,
    geo_pick,
    tint_pick,
    shade_out,
    shade_in,
    grad_out,
    grad_in,
    halo_out,
    halo_in,
    thalo_out,
    thalo_in,
    coef,
    alpha_s,
    weight_s,
    moment_s,
    send_sem,
    recv_sem,
    halo_send,
    halo_recv,
    fetch_sem,
):
    views_n, bands_n, blocks, list_len, rows, cols, block_len = geometry
    devices = views_n * bands_n
    tiles = cols // TILE
    pairs = TILE_MOST * tiles
    window = TILE_MOST * block_len
    halves = block_len // 128
    geo_rows = GEO_REC * halves
    tint_rows = 3 * halves
    hot_lanes = bands_n * blocks
    basis_lanes = BASIS * blocks
    view = lax.axis_index("view")
    band = lax.axis_index("band")
    me = band * views_n + view
    has_up = band > 0
    has_down = band < bands_n - 1

    halo_in[...] = jnp.zeros_like(halo_in)
    thalo_in[...] = jnp.zeros_like(thalo_in)
    peer_view = [lax.rem(view + d, views_n) for d in range(views_n)]
    peer_band = [lax.rem(band + d, bands_n) for d in range(bands_n)]
    barrier = pltpu.get_barrier_semaphore()
    for d in range(1, views_n):
        pl.semaphore_signal(barrier, inc=1, device_id=(peer_view[d], band), device_id_type=MESH)
    for d in range(1, bands_n):
        pl.semaphore_signal(barrier, inc=1, device_id=(view, peer_band[d]), device_id_type=MESH)

    sources = (
        (camera_hbm, camera_s),
        (list_hbm, list_s),
        (start_hbm, start_s),
        (end_hbm, end_s),
        (target_hbm, target_ref),
        (gauss_hbm, gauss_ref),
        (quad_hbm, quad_ref),
        (tone_hbm, tone_ref),
        (power_hbm, power_ref),
        (across_hbm, across_ref),
        (first_hbm, first_ref),
        (second_hbm, second_ref),
        (one_hbm, one_ref),
        (two_hbm, two_ref),
    )
    fetches = [
        pltpu.make_async_copy(source, landing, fetch_sem.at[n])
        for n, (source, landing) in enumerate(sources)
    ]
    for fetch in fetches:
        fetch.start()

    def to_all(source, landing, length, phase):
        for d_view in range(views_n):
            for d_band in range(bands_n):
                if d_view + d_band == 0:
                    continue
                peer = peer_band[d_band] * views_n + peer_view[d_view]
                pltpu.make_async_remote_copy(
                    src_ref=source.at[peer, pl.ds(0, length)],
                    dst_ref=landing.at[me, pl.ds(0, length)],
                    send_sem=send_sem.at[phase],
                    recv_sem=recv_sem.at[phase],
                    device_id=(peer_view[d_view], peer_band[d_band]),
                    device_id_type=MESH,
                ).start()

    def wait_all(landing, length, phase):
        every = landing.at[pl.ds(0, devices - 1), pl.ds(0, length)]
        pltpu.make_async_copy(every, every, recv_sem.at[phase]).wait()
        pltpu.make_async_copy(every, every, send_sem.at[phase]).wait()

    def edge_copy(source, landing, direction, phase):
        step = -1 if direction == 0 else 1
        return pltpu.make_async_remote_copy(
            src_ref=source.at[direction],
            dst_ref=landing.at[1 - direction],
            send_sem=halo_send.at[phase, direction],
            recv_sem=halo_recv.at[phase, 1 - direction],
            device_id=(view, band + step),
            device_id_type=MESH,
        )

    def edges_start(source, landing, phase):
        @pl.when(has_up)
        def _():
            edge_copy(source, landing, 0, phase).start()

        @pl.when(has_down)
        def _():
            edge_copy(source, landing, 1, phase).start()

    def edges_wait(source, landing, phase):
        @pl.when(has_up)
        def _():
            up = edge_copy(source, landing, 0, phase)
            up.wait_send()
            pltpu.make_async_copy(
                landing.at[0], landing.at[0], halo_recv.at[phase, 0]
            ).wait()

        @pl.when(has_down)
        def _():
            down = edge_copy(source, landing, 1, phase)
            down.wait_send()
            pltpu.make_async_copy(
                landing.at[1], landing.at[1], halo_recv.at[phase, 1]
            ).wait()

    def lanes_of(shape):
        return lax.broadcasted_iota(jnp.int32, shape, len(shape) - 1)

    map_lane = lanes_of((128, 128))
    map_row = lax.broadcasted_iota(jnp.int32, (128, 128), 0)
    hot_map[...] = jnp.where(
        map_row == band * blocks + lax.rem(map_lane, blocks), 1.0, 0.0
    ).astype(BF16)
    for part in range(basis_lanes // 128):
        wide_map[:, part * 128 : (part + 1) * 128] = jnp.where(
            map_row == hot_lanes + BASIS_AT + part * (128 // blocks) + map_lane // blocks, 1.0, 0.0
        ).astype(BF16)
    for kind in range(5):
        at = basis_lanes + kind * 128
        wide_map[:, at : at + 128] = jnp.where(
            (map_row == hot_lanes + TERM_ROWS * kind + map_lane // blocks)
            & (map_lane < TERM_ROWS * blocks),
            1.0,
            0.0,
        ).astype(BF16)

    fetches[0].wait()
    fetches[1].wait()
    lane = lanes_of((1, 128))
    terms = view_terms([jnp.full((1, 128), camera_s[0, c], F32) for c in range(9)])
    row = jnp.zeros((1, 128), F32)
    for n in range(TERMS):
        row = jnp.where(lane == hot_lanes + n, terms[n], row)
    wanted = lax.broadcasted_iota(jnp.int32, (views_n, 128), 0) * hot_lanes + lanes_of(
        (views_n, 128)
    )
    hits = jnp.zeros((views_n, 128), F32)
    for n in range(list_len):
        hits = jnp.where(wanted == list_s[0, 0, n], 1.0, hits)
    message = jnp.where(lanes_of((views_n, 128)) < hot_lanes, hits, row)
    for v in range(views_n):
        msg_out[v] = message[v : v + 1]

    pl.semaphore_wait(barrier, views_n + bands_n - 2)
    for d in range(1, views_n):
        pltpu.make_async_remote_copy(
            src_ref=msg_out.at[peer_view[d]],
            dst_ref=msg_in.at[me],
            send_sem=send_sem.at[0],
            recv_sem=recv_sem.at[0],
            device_id=(peer_view[d], band),
            device_id_type=MESH,
        ).start()
    msg_in[me] = msg_out[view]
    fetches[2].wait()
    fetches[3].wait()
    fetches[4].wait()
    thalo_out[0] = target_ref[0, :, 0:REACH, :]
    thalo_out[1] = target_ref[0, :, rows - REACH : rows, :]
    edges_start(thalo_out, thalo_in, 0)

    owners, alive = [], []
    for k in range(TILE_MOST):
        for t in range(tiles):
            low, high = start_s[0, 0, t], end_s[0, 0, t]
            block = list_s[0, 0, jnp.clip(jnp.minimum(low + k, high - 1), 0, list_len - 1)]
            device = lax.div(jnp.clip(block, 0, devices * blocks - 1), blocks)
            owners.append(lax.rem(device, bands_n) * views_n + lax.div(device, bands_n))
            alive.append(jnp.where(low + k < high, 1.0, 0.0))
    put_lane = lax.rem(lanes_of((devices, 2 * pairs)), pairs)
    put_row = lax.broadcasted_iota(jnp.int32, (devices, 2 * pairs), 0)
    put = jnp.zeros((devices, 2 * pairs), F32)
    for n in range(pairs):
        put = jnp.where((put_lane == n) & (put_row == owners[n]), alive[n], put)
    put = put.astype(BF16)
    tile_sub = lax.broadcasted_iota(jnp.int32, (tiles, block_len), 0)
    parts = []
    for k in range(TILE_MOST):
        part = jnp.zeros((tiles, block_len), F32)
        for t in range(tiles):
            part = jnp.where(tile_sub == t, alive[k * tiles + t], part)
        parts.append(part)
    keep = jnp.concatenate(parts, axis=1) > 0.5

    plane = msg_in.at[pl.ds(0, views_n - 1)]
    pltpu.make_async_copy(plane, plane, recv_sem.at[0]).wait()
    pltpu.make_async_copy(plane, plane, send_sem.at[0]).wait()
    bundle = msg_in.at[pl.ds(band * views_n, views_n)]
    for d in range(1, bands_n):
        pltpu.make_async_remote_copy(
            src_ref=bundle,
            dst_ref=bundle,
            send_sem=send_sem.at[1],
            recv_sem=recv_sem.at[1],
            device_id=(view, peer_band[d]),
            device_id_type=MESH,
        ).start()

    fetches[5].wait()
    (sigma, opacity), pullback = jax.vjp(
        block_shape,
        [gauss_ref[6 + c] for c in range(3)],
        [gauss_ref[9 + c] for c in range(4)],
        gauss_ref[13],
    )
    for c, value in enumerate([gauss_ref[c] for c in range(6)] + list(sigma) + [opacity]):
        geo_tab[c] = stack3(value)
    for ch in range(3):
        for q in range(BASIS):
            high, low = split2(gauss_ref[14 + 3 * q + ch])
            tint_tab[ch, 0, q * blocks : (q + 1) * blocks, :] = high
            tint_tab[ch, 1, q * blocks : (q + 1) * blocks, :] = low

    lines = msg_in.at[pl.ds(0, devices - views_n)]
    pltpu.make_async_copy(lines, lines, recv_sem.at[1]).wait()
    pltpu.make_async_copy(lines, lines, send_sem.at[1]).wait()

    asked = msg_in[...].reshape(devices, 128)
    asked_parts = split3(asked)
    hot = mx(asked_parts[0], hot_map[...])
    hot_3 = hot[:, 0 : 3 * blocks].astype(BF16)
    picked = [mx(hot_3, geo_tab[c]) for c in range(GEO_COMPS)]

    def term(n):
        return asked[:, hot_lanes + n : hot_lanes + n + 1]

    def combine(at, low):
        total = term(at) * picked[low]
        for n in range(1, TERM_ROWS):
            total = total + term(at + n) * picked[low + n]
        return total

    records = [
        combine(0, 0) + term(SHIFT_AT),
        combine(6, 0) + term(SHIFT_AT + 1),
        combine(12, 6) + 0.3,
        combine(18, 6),
        combine(24, 6) + 0.3,
        picked[12],
    ]
    geo_flat = geo_out.reshape(devices * geo_out.shape[1], 128)
    for p in range(GEO_REC):
        for h in range(halves):
            geo_flat[pl.ds(p * halves + h, devices, stride=geo_out.shape[1]), :] = records[p][
                :, h * 128 : (h + 1) * 128
            ]
    to_all(geo_out, geo_in, geo_rows, 2)
    geo_in[me] = geo_out[me]
    stacked = jnp.concatenate(asked_parts, axis=0)

    def widen(low, high):
        wide = mx(stacked, wide_map[:, low:high])
        return wide[0:devices] + wide[devices : 2 * devices] + wide[2 * devices :]

    hot_wide = jnp.concatenate([hot] * (basis_lanes // 128), axis=1)
    basis = widen(0, basis_lanes) * hot_wide
    basis_high, basis_low = split2(basis)
    basis_two = jnp.concatenate([basis_high, basis_low], axis=0)
    tint_flat = tint_out.reshape(devices * tint_out.shape[1], 128)
    for ch in range(3):
        both = mx(basis_two, tint_tab[ch, 0])
        colour = 0.5 + both[0:devices] + both[devices:] + mx(basis_high, tint_tab[ch, 1])
        for h in range(halves):
            tint_flat[pl.ds(ch * halves + h, devices, stride=tint_out.shape[1]), :] = colour[
                :, h * 128 : (h + 1) * 128
            ]
    to_all(tint_out, tint_in, tint_rows, 3)
    tint_in[me] = tint_out[me]

    tint_back[...] = jnp.concatenate([basis_high, basis_low, basis_high], axis=0)
    spans = [
        widen(basis_lanes + kind * 128, basis_lanes + (kind + 1) * 128) * hot for kind in range(5)
    ]
    hot_lane = lanes_of((devices, 128))
    hot_last = jnp.where(
        (hot_lane >= TERM_ROWS * blocks) & (hot_lane < (TERM_ROWS + 1) * blocks), hot, 0.0
    )
    for landing, group in ((line_back, spans[0:2] + [hot_last]), (shape_back, spans[2:5])):
        high, low = split2(jnp.concatenate(group, axis=0))
        landing[...] = jnp.concatenate([high, low, high], axis=0)

    for n in range(6, 12):
        fetches[n].wait()
    edges_wait(thalo_out, thalo_in, 0)
    in_rows, mid_rows = up8(rows + 2 * REACH), up8(rows + REACH)
    high_rows = 3 * mid_rows
    fill = jnp.zeros((in_rows - rows - 2 * REACH, cols), F32)

    def smooth(fields):
        down = jnp.dot(
            first_ref[...],
            jnp.concatenate(fields, axis=1),
            precision=HIGHEST_MODE,
            preferred_element_type=F32,
        )
        stack = jnp.concatenate(
            [down[:, f * cols : (f + 1) * cols] for f in range(len(fields))], axis=0
        )
        flat = jnp.dot(
            stack, across_ref[...], precision=HIGHEST_MODE, preferred_element_type=F32
        )
        return [flat[f * high_rows : (f + 1) * high_rows] for f in range(len(fields))]

    mine = target_ref[0]
    ext_y = jnp.concatenate(
        [v for ch in range(3) for v in (thalo_in[0, ch], mine[ch], thalo_in[1, ch], fill)], axis=0
    )
    mean_y, square_y = smooth([ext_y, ext_y * ext_y])

    wait_all(geo_in, geo_rows, 2)
    for k in range(TILE_MOST):
        for t in range(tiles):
            geo_pick[k, pl.ds(t, geo_rows, stride=tiles), :] = geo_in[
                owners[k * tiles + t], 0:geo_rows, :
            ]

    def gathered(landed, p):
        return jnp.concatenate(
            [
                landed[k, (p * halves + h) * tiles : (p * halves + h + 1) * tiles, :]
                for k in range(TILE_MOST)
                for h in range(halves)
            ],
            axis=1,
        )

    tile_row = lax.broadcasted_iota(jnp.int32, (tiles, window), 0).astype(F32)
    u_rel = gathered(geo_pick, 0) - (tile_row * TILE + 0.5 * TILE)
    w_rel = gathered(geo_pick, 1) - ((band * rows).astype(F32) + 0.5 * TILE)
    c_a = gathered(geo_pick, 2)
    c_b = gathered(geo_pick, 3)
    c_c = gathered(geo_pick, 4)
    opac = gathered(geo_pick, 5)
    inv_det = 1.0 / (c_a * c_c - c_b * c_b)
    coef_a = -0.5 * c_c * inv_det
    coef_b = c_b * inv_det
    coef_c = -0.5 * c_a * inv_det

    def masked(value, other=0.0):
        return jnp.where(keep, value, other)

    flat = LOG2_E * (
        coef_a * u_rel * u_rel + coef_b * u_rel * w_rel + coef_c * w_rel * w_rel
    ) + LOG2_E * jnp.log(opac)
    quads = jnp.concatenate(
        [
            masked(flat, NEVER),
            masked(LOG2_E * (-2.0 * coef_a * u_rel - coef_b * w_rel)),
            masked(LOG2_E * coef_a),
            masked(LOG2_E * (-coef_b * u_rel - 2.0 * coef_c * w_rel)),
            masked(LOG2_E * coef_b),
            masked(LOG2_E * coef_c),
        ],
        axis=0,
    )
    grown = mx(stack3(quads), quad_ref[...], TN)
    for n in range(3):
        coef[n] = grown[:, n * cols : (n + 1) * cols]
    wait_all(tint_in, tint_rows, 3)
    for k in range(TILE_MOST):
        for t in range(tiles):
            tint_pick[k, pl.ds(t, tint_rows, stride=tiles), :] = tint_in[
                owners[k * tiles + t], 0:tint_rows, :
            ]
    tones = jnp.concatenate([masked(gathered(tint_pick, ch)) for ch in range(3)], axis=0)
    grown = mx(stack2(tones), tone_ref[...], TN)
    for ch in range(3):
        coef[3 + ch] = grown[:, ch * cols : (ch + 1) * cols]

    sub8 = lax.broadcasted_iota(jnp.int32, (8, cols), 0).astype(F32)
    parts_n = rows // 8
    row_local = [sub8 + (8.0 * part + 0.5 - 0.5 * TILE) for part in range(parts_n)]

    def spread_row(kind, j):
        return coef[kind, pl.ds(j, 8, stride=0), :]

    def blend(group, carry):
        trans, image = carry
        trans, image = list(trans), list(image)
        for k in range(8):
            j = group * 8 + k
            q0, q1, q2 = spread_row(0, j), spread_row(1, j), spread_row(2, j)
            tint = [spread_row(3 + ch, j) for ch in range(3)]
            for part in range(parts_n):
                r = row_local[part]
                alpha = jnp.exp2(q0 + r * (q1 + r * q2))
                weight = alpha * trans[part]
                alpha_s[j, part] = alpha
                weight_s[j, part] = weight
                trans[part] = trans[part] * (1.0 - alpha)
                for ch in range(3):
                    at = ch * parts_n + part
                    image[at] = image[at] + weight * tint[ch]
        return tuple(trans), tuple(image)

    zero = jnp.zeros((8, cols), F32)
    _, image = lax.fori_loop(
        0,
        window // 8,
        blend,
        (tuple([zero + 1.0] * parts_n), tuple([zero] * (3 * parts_n))),
    )
    pred = [
        jnp.concatenate([image[ch * parts_n + part] for part in range(parts_n)], axis=0)
        for ch in range(3)
    ]
    for ch in range(3):
        halo_out[0, ch] = pred[ch][0:REACH]
        halo_out[1, ch] = pred[ch][rows - REACH : rows]
    edges_start(halo_out, halo_in, 1)
    edges_wait(halo_out, halo_in, 1)

    ext_x = jnp.concatenate(
        [v for ch in range(3) for v in (halo_in[0, ch], pred[ch], halo_in[1, ch], fill)], axis=0
    )
    mean_x, square_x, cross = smooth([ext_x, ext_x * ext_x, ext_x * ext_y])
    n_mean = 2.0 * mean_x * mean_y + STAB_MEAN
    n_var = 2.0 * (cross - mean_x * mean_y) + STAB_VAR
    d_mean = mean_x * mean_x + mean_y * mean_y + STAB_MEAN
    d_var = (square_x - mean_x * mean_x) + (square_y - mean_y * mean_y) + STAB_VAR
    inv_mean = 1.0 / d_mean
    inv_var = 1.0 / d_var
    inverse = inv_mean * inv_var
    ssim = n_mean * n_var * inverse
    ext_row = lax.broadcasted_iota(jnp.int32, (high_rows, cols), 0) % mid_rows
    image_row = ext_row + (band * rows - HALO)
    inside = (image_row >= 0) & (image_row < bands_n * rows) & (ext_row < rows + REACH)
    scale = -SSIM_WEIGHT / 3.0
    part_mean = 2.0 * mean_y * (n_var - n_mean) * inverse - 2.0 * mean_x * ssim * (
        inv_mean - inv_var
    )
    adjoint = jnp.concatenate(
        [
            jnp.where(inside, scale * part_mean, 0.0),
            jnp.where(inside, -scale * ssim * inv_var, 0.0),
            jnp.where(inside, (2.0 * scale) * n_mean * inverse, 0.0),
        ],
        axis=1,
    )
    down2 = jnp.dot(second_ref[...], adjoint, precision=HIGHEST_MODE, preferred_element_type=F32)
    stacked2 = jnp.concatenate([down2[:, f * cols : (f + 1) * cols] for f in range(3)], axis=0)
    spread = jnp.dot(
        stacked2, across_ref[...], precision=HIGHEST_MODE, preferred_element_type=F32
    )
    deep = 3 * rows
    pred_all = jnp.concatenate(pred, axis=0)
    mine_all = jnp.concatenate([mine[ch] for ch in range(3)], axis=0)
    error = pred_all - mine_all
    sign = jnp.where(error > 0.0, 1.0, jnp.where(error < 0.0, -1.0, 0.0))
    grad_pred = (
        ABS_WEIGHT / 3.0 * sign
        + spread[0:deep]
        + 2.0 * pred_all * spread[deep : 2 * deep]
        + mine_all * spread[2 * deep : 3 * deep]
    )
    own = (ext_row >= HALO) & (ext_row < HALO + rows)
    loss = jnp.sum(ABS_WEIGHT / 3.0 * jnp.abs(error), keepdims=True) + jnp.sum(
        jnp.where(own, SSIM_WEIGHT / 3.0 * (1.0 - ssim), 0.0), keepdims=True
    )

    pull = [
        [grad_pred[ch * rows + 8 * part : ch * rows + 8 * part + 8] for part in range(parts_n)]
        for ch in range(3)
    ]

    def shades(group, carry):
        sums = [[None] * 8 for _ in range(3)]
        for k in range(8):
            j = group * 8 + k
            weight = [weight_s[j, part] for part in range(parts_n)]
            for ch in range(3):
                total = weight[0] * pull[ch][0]
                for part in range(1, parts_n):
                    total = total + weight[part] * pull[ch][part]
                sums[ch][k] = total
        at = pl.multiple_of(group * 8, 8)
        for ch in range(3):
            moment_s[3 + ch, pl.ds(at, 8), :] = tree_sum(sums[ch], cols)
        return carry

    lax.fori_loop(0, window // 8, shades, 0)

    def route(value):
        stack = jnp.concatenate(
            [value[:, k * block_len : (k + 1) * block_len] for k in range(TILE_MOST)], axis=0
        )
        return mx(put, stack2(stack))

    power = power_ref[...]
    shade_flat = shade_out.reshape(devices * shade_out.shape[1], 128)
    for ch in range(3):
        routed = route(exact_dot(power[0:tiles], moment_s[3 + ch], NT))
        for h in range(halves):
            shade_flat[pl.ds(ch * halves + h, devices, stride=shade_out.shape[1]), :] = routed[
                :, h * 128 : (h + 1) * 128
            ]
    shade_flat[pl.ds(tint_rows, devices, stride=shade_out.shape[1]), :] = jnp.broadcast_to(
        loss, (devices, 128)
    )
    to_all(shade_out, shade_in, tint_rows + 1, 4)
    shade_in[me] = shade_out[me]

    def unblend(step, behind):
        group = window // 8 - 1 - step
        behind = list(behind)
        sums = [[None] * 8 for _ in range(3)]
        for k in reversed(range(8)):
            j = group * 8 + k
            tint = [spread_row(3 + ch, j) for ch in range(3)]
            totals = [None] * 3
            for part in range(parts_n):
                alpha = alpha_s[j, part]
                shade = (
                    tint[0] * pull[0][part] + tint[1] * pull[1][part] + tint[2] * pull[2][part]
                )
                gap = shade - behind[part]
                behind[part] = alpha * shade + (1.0 - alpha) * behind[part]
                lean = weight_s[j, part] * gap
                lean_r = lean * row_local[part]
                terms = [lean, lean_r, lean_r * row_local[part]]
                totals = [
                    value if total is None else total + value
                    for value, total in zip(terms, totals)
                ]
            for kind in range(3):
                sums[kind][k] = totals[kind]
        at = pl.multiple_of(group * 8, 8)
        for kind in range(3):
            moment_s[kind, pl.ds(at, 8), :] = tree_sum(sums[kind], cols)
        return tuple(behind)

    lax.fori_loop(0, window // 8, unblend, tuple([zero] * parts_n))

    by_x = exact_dot(power, moment_s[0], NT)
    m_00, m_10, m_20 = by_x[0:tiles], by_x[tiles : 2 * tiles], by_x[2 * tiles : 3 * tiles]
    by_xr = exact_dot(power[0 : 2 * tiles], moment_s[1], NT)
    m_01, m_11 = by_xr[0:tiles], by_xr[tiles : 2 * tiles]
    m_02 = exact_dot(power[0:tiles], moment_s[2], NT)
    s_x = m_10 - u_rel * m_00
    s_y = m_01 - w_rel * m_00
    s_xx = m_20 - 2.0 * u_rel * m_10 + u_rel * u_rel * m_00
    s_xy = m_11 - u_rel * m_01 - w_rel * m_10 + u_rel * w_rel * m_00
    s_yy = m_02 - 2.0 * w_rel * m_01 + w_rel * w_rel * m_00
    by_det = -(coef_a * s_xx + coef_b * s_xy + coef_c * s_yy) * inv_det
    derivs = [
        -(2.0 * coef_a * s_x + coef_b * s_y),
        -(2.0 * coef_c * s_y + coef_b * s_x),
        -0.5 * inv_det * s_yy + by_det * c_c,
        inv_det * s_xy - 2.0 * c_b * by_det,
        -0.5 * inv_det * s_xx + by_det * c_a,
        m_00 / opac,
    ]
    grad_flat = grad_out.reshape(devices * grad_out.shape[1], 128)
    for p in range(GEO_REC):
        routed = route(derivs[p])
        for h in range(halves):
            grad_flat[pl.ds(p * halves + h, devices, stride=grad_out.shape[1]), :] = routed[
                :, h * 128 : (h + 1) * 128
            ]
    to_all(grad_out, grad_in, geo_rows, 5)
    grad_in[me] = grad_out[me]

    wait_all(shade_in, tint_rows + 1, 4)
    shade_back = shade_in.reshape(devices * shade_in.shape[1], 128)
    grad_back = grad_in.reshape(devices * grad_in.shape[1], 128)

    def arrived(landed, stride, p):
        return jnp.concatenate(
            [landed[pl.ds(p * halves + h, devices, stride=stride), :] for h in range(halves)],
            axis=1,
        )

    def spread_back(table, values):
        high, low = split2(jnp.concatenate(values, axis=0))
        return mx(table[...], jnp.concatenate([high, high, low], axis=0), TN)

    for ch in range(3):
        colour = spread_back(tint_back, [arrived(shade_back, shade_in.shape[1], ch)])
        for q in range(BASIS):
            grad_ref[14 + 3 * q + ch] = colour[q * blocks : (q + 1) * blocks]
    losses = shade_back[pl.ds(tint_rows, devices, stride=shade_in.shape[1]), :]
    loss_ref[...] = jnp.sum(losses, axis=0, keepdims=True)[:, 0:1] * (
        1.0 / (devices * rows * cols)
    )
    fetches[12].wait()
    fetches[13].wait()

    wait_all(grad_in, geo_rows, 5)
    geos = [arrived(grad_back, grad_in.shape[1], p) for p in range(GEO_REC)]
    line = spread_back(line_back, [geos[0], geos[1], geos[5]])
    shape = spread_back(shape_back, geos[2:5])

    def comp(value, n):
        return value[n * blocks : (n + 1) * blocks]

    d_logs, d_quats, d_logit = pullback(
        ([comp(shape, n) for n in range(TERM_ROWS)], comp(line, TERM_ROWS))
    )
    columns = [comp(line, n) for n in range(TERM_ROWS)] + list(d_logs) + list(d_quats) + [d_logit]
    for c, value in enumerate(columns):
        grad_ref[c] = value


def adam_kernel(
    grad_ref,
    gauss_ref,
    one_ref,
    two_ref,
    loss_in,
    out_gauss,
    out_one,
    out_two,
    out_grad,
    loss_out,
    gauss_v,
    one_v,
    two_v,
    write_sem,
):
    whole = pltpu.make_async_copy(grad_ref, out_grad, write_sem.at[3, 0])
    whole.start()
    total = pltpu.make_async_copy(loss_in, loss_out, write_sem.at[3, 1])
    total.start()
    comps = gauss_ref.shape[0]
    pieces = [whole, total]
    for piece in range(PIECES):
        low, high = piece * comps // PIECES, (piece + 1) * comps // PIECES

        def update(c, carry):
            gradient = grad_ref[c]
            new_one = 0.9 * one_ref[c] + 0.1 * gradient
            new_two = 0.999 * two_ref[c] + 0.001 * gradient * gradient
            one_v[c] = new_one
            two_v[c] = new_two
            bottom = jnp.sqrt(new_two * (1.0 / BIAS_SECOND)) + 1e-08
            gauss_v[c] = gauss_ref[c] - learning_rate(c) * new_one / bottom
            return carry

        lax.fori_loop(low, high, update, 0, unroll=2)
        part = pl.ds(low, high - low)
        for source, landing, sem in (
            (one_v, out_one, 0),
            (two_v, out_two, 1),
            (gauss_v, out_gauss, 2),
        ):
            copy = pltpu.make_async_copy(
                source.at[part], landing.at[part], write_sem.at[sem, piece]
            )
            copy.start()
            pieces.append(copy)
    for copy in pieces:
        copy.wait()


def quad_table(tiles, cols):
    lane = np.arange(cols)
    local = lane % TILE + 0.5 - TILE / 2
    belongs = (lane[None, :] // TILE == np.arange(tiles)[:, None]).astype(np.float32)
    nothing = np.zeros_like(belongs)
    rows = [
        [belongs, nothing, nothing],
        [belongs * local, nothing, nothing],
        [belongs * local * local, nothing, nothing],
        [nothing, belongs, nothing],
        [nothing, belongs * local, nothing],
        [nothing, nothing, belongs],
    ]
    return np.tile(np.block(rows), (3, 1))


def tone_table(tiles, cols):
    belongs = (np.arange(cols)[None, :] // TILE == np.arange(tiles)[:, None]).astype(np.float32)
    return np.tile(np.kron(np.eye(3, dtype=np.float32), belongs), (2, 1))


def per_device(
    gaussians,
    first_moment,
    second_moment,
    camera,
    target,
    block_list,
    block_count,
    tile_start,
    tile_end,
):
    views_n = lax.axis_size("view")
    bands_n = lax.axis_size("band")
    devices = views_n * bands_n
    blocks, comps, block_len = gaussians.shape
    list_len = block_list.shape[2]
    rows, cols = target.shape[2:]
    tiles = cols // TILE
    halves = block_len // 128
    geometry = (views_n, bands_n, blocks, list_len, rows, cols, block_len)

    across, first, second = smoothing_tables(rows, cols, 3)
    power = power_table(tiles, cols)
    quad = quad_table(tiles, cols).astype(BF16)
    tone = tone_table(tiles, cols).astype(BF16)
    vmem = pl.BlockSpec(memory_space=pltpu.VMEM)
    hbm = pl.BlockSpec(memory_space=pltpu.HBM)

    def by_comp(array):
        return jnp.transpose(array, (1, 0, 2))

    window = TILE_MOST * block_len
    geo_pad, tint_pad = up8(GEO_REC * halves), up8(3 * halves + 1)
    basis_lanes = BASIS * blocks
    shape = jax.ShapeDtypeStruct((comps, blocks, block_len), F32)
    scalar = jax.ShapeDtypeStruct((1, 1), F32)
    kept = pltpu.VMEM(shape.shape, F32)
    gradient, params, one, two, mean_loss = pl.pallas_call(
        functools.partial(step_kernel, geometry),
        out_shape=(kept, kept, kept, kept, pltpu.VMEM((1, 1), F32)),
        in_specs=[hbm] * 14,
        out_specs=(vmem,) * 5,
        scratch_shapes=[
            pltpu.SMEM((1, 9), F32),
            pltpu.SMEM((1, 1, list_len), jnp.int32),
            pltpu.SMEM((1, 1, tiles), jnp.int32),
            pltpu.SMEM((1, 1, tiles), jnp.int32),
            pltpu.VMEM((1, 3, rows, cols), F32),
            pltpu.VMEM(across.shape, F32),
            pltpu.VMEM(first.shape, F32),
            pltpu.VMEM(second.shape, F32),
            pltpu.VMEM(power.shape, F32),
            pltpu.VMEM(quad.shape, BF16),
            pltpu.VMEM(tone.shape, BF16),
            pltpu.VMEM((views_n, 1, 128), F32),
            pltpu.VMEM((devices, 1, 128), F32),
            pltpu.VMEM((128, 128), BF16),
            pltpu.VMEM((128, basis_lanes + 5 * 128), BF16),
            pltpu.VMEM((GEO_COMPS, 3 * blocks, block_len), BF16),
            pltpu.VMEM((3, 2, basis_lanes, block_len), BF16),
            pltpu.VMEM((3 * devices, basis_lanes), BF16),
            pltpu.VMEM((9 * devices, 128), BF16),
            pltpu.VMEM((9 * devices, 128), BF16),
            pltpu.VMEM((devices, geo_pad, 128), F32),
            pltpu.VMEM((devices, geo_pad, 128), F32),
            pltpu.VMEM((devices, tint_pad, 128), F32),
            pltpu.VMEM((devices, tint_pad, 128), F32),
            pltpu.VMEM((TILE_MOST, GEO_REC * halves * tiles, 128), F32),
            pltpu.VMEM((TILE_MOST, 3 * halves * tiles, 128), F32),
            pltpu.VMEM((devices, tint_pad, 128), F32),
            pltpu.VMEM((devices, tint_pad, 128), F32),
            pltpu.VMEM((devices, geo_pad, 128), F32),
            pltpu.VMEM((devices, geo_pad, 128), F32),
            pltpu.VMEM((2, 3, REACH, cols), F32),
            pltpu.VMEM((2, 3, REACH, cols), F32),
            pltpu.VMEM((2, 3, REACH, cols), F32),
            pltpu.VMEM((2, 3, REACH, cols), F32),
            pltpu.VMEM((6, window, cols), F32),
            pltpu.VMEM((window, rows // 8, 8, cols), F32),
            pltpu.VMEM((window, rows // 8, 8, cols), F32),
            pltpu.VMEM((6, window, cols), F32),
            pltpu.SemaphoreType.DMA((6,)),
            pltpu.SemaphoreType.DMA((6,)),
            pltpu.SemaphoreType.DMA((2, 2)),
            pltpu.SemaphoreType.DMA((2, 2)),
            pltpu.SemaphoreType.DMA((14,)),
        ],
        compiler_params=pltpu.CompilerParams(
            collective_id=0, has_side_effects=True, vmem_limit_bytes=40 * 1024 * 1024
        ),
        name="render_step",
    )(
        *[
            pltpu.with_memory_space_constraint(array, pltpu.HBM)
            for array in (
                camera,
                block_list,
                tile_start,
                tile_end,
                target,
                by_comp(gaussians),
                by_comp(first_moment),
                by_comp(second_moment),
                across,
                first,
                second,
                power,
                quad,
                tone,
            )
        ]
    )

    new_params, new_one, new_two, out_gradient, out_loss = pl.pallas_call(
        adam_kernel,
        out_shape=(shape, shape, shape, shape, scalar),
        in_specs=[vmem] * 5,
        out_specs=(hbm, hbm, hbm, hbm, hbm),
        scratch_shapes=[pltpu.VMEM((comps, blocks, block_len), F32)] * 3
        + [pltpu.SemaphoreType.DMA((4, PIECES))],
        compiler_params=pltpu.CompilerParams(vmem_limit_bytes=16 * 1024 * 1024),
        name="adam_step",
    )(gradient, params, one, two, mean_loss)
    return (
        by_comp(new_params),
        by_comp(new_one),
        by_comp(new_two),
        out_loss.reshape(()),
        by_comp(out_gradient),
    )


def solution(mesh):
    return jax.shard_map(
        per_device,
        mesh=mesh,
        in_specs=(
            P(("view", "band"), None, None),
            P(("view", "band"), None, None),
            P(("view", "band"), None, None),
            P("view", None),
            P("view", None, "band", None),
            P("view", "band", None),
            P("view", "band"),
            P("view", "band", None),
            P("view", "band", None),
        ),
        out_specs=(
            P(("view", "band"), None, None),
            P(("view", "band"), None, None),
            P(("view", "band"), None, None),
            P(),
            P(("view", "band"), None, None),
        ),
        check_vma=False,
    )
```

time: 50.6 us -> 46.3 us (0.915)
  Pallas kernels: 49.8 us -> 45.5 us
    pallas_call x2, Pallas kernels: 49.8 us -> 45.5 us  [the longest x1 42.7 us: per_device(): pl.pallas_call(functools.partial(step_kernel, geometry), out_shape=(kept,...]
where the time goes in v1:
time: 46.3 us; the launch traced here: 46.1 us
  Pallas kernels  45.5 us (98%)
  between operations  0.64 us (1%)
    pallas_call x1, Pallas kernels, per_device(): pl.pallas_call(functools.partial(step_kernel, geometry), out_shape=(kept,...  42.7 us
    pallas_call x1, Pallas kernels, per_device(): pl.pallas_call(adam_kernel, out_shape=(shape, shape, shape, shape, scalar...  2.76 us

profile of v1, /device:TPU:0, one launch (start us, length us, event | category | flops | bytes accessed | tf_op | source)
XLA Modules:
  0.0 46.1 jit_solution(8438905933297662651)
XLA Ops:
  0.6 42.7 %render_step.1 = (f32[62,16,256]{2,1,0:T(8,128)S(1)}, f32[62,16,256]{2,1,0:T(8,128)S(1)}, f32[62,16,256]{2,1,0:T(8,128)S(1)}, f32[62,16,256]{2,1,0:T(8,128)S(1)}, f32[1,1]{1,0:T(1,128)}) custom-call(f32[1,9]{1,0:T(1,128)} %camera_hbm.1, s32[1,1,16]{2,1,0:T(1,128)} %list_hbm.1, s32[1,1,8]{2,1,0:T(1,128)} %start_hbm.1, s32[1,1,8]{2,1,0:T(1,128)} %end_hbm.1, ...), custom_call_target="tpu_custom_call" | custom-call | tf_op jit(solution)/shard_map/render_step/pallas_call | solution.py:1010
  43.4 2.8 %adam_step.1 = (f32[62,16,256]{2,1,0:T(8,128)}, f32[62,16,256]{2,1,0:T(8,128)}, f32[62,16,256]{2,1,0:T(8,128)}, f32[62,16,256]{2,1,0:T(8,128)}, f32[1,1]{1,0:T(1,128)}) custom-call(f32[62,16,256]{2,1,0:T(8,128)S(1)} %get-tuple-element.15.grad_ref, f32[62,16,256]{2,1,0:T(8,128)S(1)} %get-tuple-element.16.gauss_ref, ...), custom_call_target="tpu_custom_call" | custom-call | tf_op jit(solution)/shard_map/adam_step/pallas_call | solution.py:1086

commit v2 on v1

--- a/solution.py
+++ b/solution.py
@@ -14,7 +14,10 @@
 HALO = 5
 REACH = 2 * HALO
 GEO_REC = 6
-PIECES = 4
+RECORDS = 9
+PIECES = 3
+SHAPE_COMPS = 14
+UNROLL = 4
 
 HIGHEST_MODE = lax.Precision.HIGHEST
 SSIM_WEIGHT = 0.2
@@ -53,6 +56,8 @@
 
 def learning_rate(component):
     rate = RATES[-1][1] / BIAS_FIRST
+    if isinstance(component, int):
+        return next(value for end, value in RATES if component < end) / BIAS_FIRST
     for end, value in reversed(RATES[:-1]):
         rate = jnp.where(component < end, value / BIAS_FIRST, rate)
     return rate
@@ -186,9 +191,18 @@
     return join(z1, z2, (sub % 2) < 1, 1)
 
 
-def block_shape(logs, quats, logit):
-    squares = [jnp.exp(value) for value in logs]
-    squares = [value * value for value in squares]
+def adam_step(c, grad_ref, source, landing):
+    gradient = grad_ref[c]
+    new_one = 0.9 * source[1][c] + 0.1 * gradient
+    new_two = 0.999 * source[2][c] + 0.001 * gradient * gradient
+    landing[1][c] = new_one
+    landing[2][c] = new_two
+    bottom = jnp.sqrt(new_two * (1.0 / BIAS_SECOND)) + 1e-08
+    landing[0][c] = source[0][c] - learning_rate(c) * new_one / bottom
+
+
+def block_axes(logs, quats):
+    scales = [jnp.exp(value) for value in logs]
     quat_len = jnp.sqrt(
         quats[0] * quats[0] + quats[1] * quats[1] + quats[2] * quats[2] + quats[3] * quats[3]
     )
@@ -198,14 +212,15 @@
         [2.0 * (i * j + r * k), 1.0 - 2.0 * (i * i + k * k), 2.0 * (j * k - r * i)],
         [2.0 * (i * k - r * j), 2.0 * (j * k + r * i), 1.0 - 2.0 * (i * i + j * j)],
     ]
-    spread = [[rotation[a][c] * squares[c] for c in range(3)] for a in range(3)]
+    return rotation, scales
+
+
+def block_shape(logs, quats, logit):
+    rotation, scales = block_axes(logs, quats)
+    axes = [[rotation[a][c] * scales[c] for c in range(3)] for a in range(3)]
 
     def moment(a, b):
-        return (
-            spread[a][0] * rotation[b][0]
-            + spread[a][1] * rotation[b][1]
-            + spread[a][2] * rotation[b][2]
-        )
+        return axes[a][0] * axes[b][0] + axes[a][1] * axes[b][1] + axes[a][2] * axes[b][2]
 
     pairs = ((0, 0), (1, 1), (2, 2), (0, 1), (0, 2), (1, 2))
     return [moment(a, b) for a, b in pairs], 1.0 / (1.0 + jnp.exp(-logit))
@@ -218,15 +233,15 @@
     terms += [a[c] * a[c] for c in range(3)] + [2.0 * a[c] * a[d] for c, d in crossed]
     terms += [a[c] * b[c] for c in range(3)] + [a[c] * b[d] + a[d] * b[c] for c, d in crossed]
     terms += [b[c] * b[c] for c in range(3)] + [2.0 * b[c] * b[d] for c, d in crossed]
-    return terms + [cam[6], cam[7]] + camera_basis(cam[0:6])
+    return terms + [cam[6], cam[7], time] + camera_basis(cam[0:6])
 
 
 TERM_ROWS = 6
 SHIFT_AT = 30
-BASIS_AT = 32
+BASIS_AT = 33
 BASIS = 16
-TERMS = 48
-GEO_COMPS = 13
+TERMS = 49
+GEO_COMPS = 19
 
 
 def step_kernel(
@@ -258,11 +273,14 @@
     across_ref,
     first_ref,
     second_ref,
+    second_k,
+    across_k,
     power_ref,
     quad_ref,
     tone_ref,
     msg_out,
     msg_in,
+    asked_ref,
     hot_map,
     wide_map,
     geo_tab,
@@ -270,12 +288,9 @@
     tint_back,
     line_back,
     shape_back,
-    geo_out,
-    geo_in,
-    tint_out,
-    tint_in,
-    geo_pick,
-    tint_pick,
+    rec_out,
+    rec_in,
+    rec_pick,
     shade_out,
     shade_in,
     grad_out,
@@ -300,7 +315,7 @@
     pairs = TILE_MOST * tiles
     window = TILE_MOST * block_len
     halves = block_len // 128
-    geo_rows = GEO_REC * halves
+    pair_len = TILE_MOST * 128
     tint_rows = 3 * halves
     hot_lanes = bands_n * blocks
     basis_lanes = BASIS * blocks
@@ -470,10 +485,10 @@
     for n in range(pairs):
         put = jnp.where((put_lane == n) & (put_row == owners[n]), alive[n], put)
     put = put.astype(BF16)
-    tile_sub = lax.broadcasted_iota(jnp.int32, (tiles, block_len), 0)
+    tile_sub = lax.broadcasted_iota(jnp.int32, (tiles, 128), 0)
     parts = []
     for k in range(TILE_MOST):
-        part = jnp.zeros((tiles, block_len), F32)
+        part = jnp.zeros((tiles, 128), F32)
         for t in range(tiles):
             part = jnp.where(tile_sub == t, alive[k * tiles + t], part)
         parts.append(part)
@@ -500,49 +515,38 @@
         [gauss_ref[9 + c] for c in range(4)],
         gauss_ref[13],
     )
-    for c, value in enumerate([gauss_ref[c] for c in range(6)] + list(sigma) + [opacity]):
-        geo_tab[c] = stack3(value)
+    rotation, scales = block_axes(
+        [gauss_ref[6 + c] for c in range(3)], [gauss_ref[9 + c] for c in range(4)]
+    )
+    tabled = [gauss_ref[c] for c in range(6)] + [v for line in rotation for v in line] + scales
+    for c, value in enumerate(tabled + [opacity]):
+        both = stack3(value)
+        for h in range(halves):
+            geo_tab[h, c] = both[:, h * 128 : (h + 1) * 128]
     for ch in range(3):
         for q in range(BASIS):
-            high, low = split2(gauss_ref[14 + 3 * q + ch])
-            tint_tab[ch, 0, q * blocks : (q + 1) * blocks, :] = high
-            tint_tab[ch, 1, q * blocks : (q + 1) * blocks, :] = low
+            for n, piece in enumerate(split3(gauss_ref[14 + 3 * q + ch])):
+                for h in range(halves):
+                    tint_tab[
+                        h, n, q * blocks : (q + 1) * blocks, ch * 128 : (ch + 1) * 128
+                    ] = piece[:, h * 128 : (h + 1) * 128]
 
     lines = msg_in.at[pl.ds(0, devices - views_n)]
     pltpu.make_async_copy(lines, lines, recv_sem.at[1]).wait()
     pltpu.make_async_copy(lines, lines, send_sem.at[1]).wait()
 
-    asked = msg_in[...].reshape(devices, 128)
+    for p in range(devices):
+        asked_ref[p : p + 1, :] = msg_in[p]
+    asked = asked_ref[...]
     asked_parts = split3(asked)
     hot = mx(asked_parts[0], hot_map[...])
     hot_3 = hot[:, 0 : 3 * blocks].astype(BF16)
-    picked = [mx(hot_3, geo_tab[c]) for c in range(GEO_COMPS)]
 
     def term(n):
         return asked[:, hot_lanes + n : hot_lanes + n + 1]
 
-    def combine(at, low):
-        total = term(at) * picked[low]
-        for n in range(1, TERM_ROWS):
-            total = total + term(at + n) * picked[low + n]
-        return total
-
-    records = [
-        combine(0, 0) + term(SHIFT_AT),
-        combine(6, 0) + term(SHIFT_AT + 1),
-        combine(12, 6) + 0.3,
-        combine(18, 6),
-        combine(24, 6) + 0.3,
-        picked[12],
-    ]
-    geo_flat = geo_out.reshape(devices * geo_out.shape[1], 128)
-    for p in range(GEO_REC):
-        for h in range(halves):
-            geo_flat[pl.ds(p * halves + h, devices, stride=geo_out.shape[1]), :] = records[p][
-                :, h * 128 : (h + 1) * 128
-            ]
-    to_all(geo_out, geo_in, geo_rows, 2)
-    geo_in[me] = geo_out[me]
+    ones = [term(c) for c in range(3)], [term(TERM_ROWS + c) for c in range(3)]
+    shifts = [term(SHIFT_AT), term(SHIFT_AT + 1), term(SHIFT_AT + 2)]
     stacked = jnp.concatenate(asked_parts, axis=0)
 
     def widen(low, high):
@@ -550,21 +554,44 @@
         return wide[0:devices] + wide[devices : 2 * devices] + wide[2 * devices :]
 
     hot_wide = jnp.concatenate([hot] * (basis_lanes // 128), axis=1)
-    basis = widen(0, basis_lanes) * hot_wide
-    basis_high, basis_low = split2(basis)
-    basis_two = jnp.concatenate([basis_high, basis_low], axis=0)
-    tint_flat = tint_out.reshape(devices * tint_out.shape[1], 128)
-    for ch in range(3):
-        both = mx(basis_two, tint_tab[ch, 0])
-        colour = 0.5 + both[0:devices] + both[devices:] + mx(basis_high, tint_tab[ch, 1])
-        for h in range(halves):
-            tint_flat[pl.ds(ch * halves + h, devices, stride=tint_out.shape[1]), :] = colour[
-                :, h * 128 : (h + 1) * 128
-            ]
-    to_all(tint_out, tint_in, tint_rows, 3)
-    tint_in[me] = tint_out[me]
-
-    tint_back[...] = jnp.concatenate([basis_high, basis_low, basis_high], axis=0)
+    basis_parts = split3(widen(0, basis_lanes) * hot_wide)
+    basis_three = jnp.concatenate(basis_parts, axis=0)
+
+    def records_of(h):
+        picked = [mx(hot_3, geo_tab[h, c]) for c in range(GEO_COMPS)]
+        centre = [picked[c] + shifts[2] * picked[3 + c] for c in range(3)]
+        turns, scales = [picked[6 + 3 * a : 9 + 3 * a] for a in range(3)], picked[15:18]
+
+        def placed(row, shift):
+            return row[0] * centre[0] + row[1] * centre[1] + row[2] * centre[2] + shift
+
+        def turned(row, c):
+            return (row[0] * turns[0][c] + row[1] * turns[1][c] + row[2] * turns[2][c]) * scales[c]
+
+        m = [[turned(row, c) for c in range(3)] for row in ones]
+        small = mx(basis_parts[0], tint_tab[h, 2])
+        middle = mx(basis_three[0 : 2 * devices], tint_tab[h, 1])
+        large = mx(basis_three, tint_tab[h, 0])
+        colour = small + large[2 * devices :] + middle[devices:]
+        colour = colour + (middle[0:devices] + large[devices : 2 * devices])
+        colour = 0.5 + (colour + large[0:devices])
+        return [
+            placed(ones[0], shifts[0]),
+            placed(ones[1], shifts[1]),
+            m[0][0] * m[0][0] + m[0][1] * m[0][1] + m[0][2] * m[0][2] + 0.3,
+            m[0][0] * m[1][0] + m[0][1] * m[1][1] + m[0][2] * m[1][2],
+            m[1][0] * m[1][0] + m[1][1] * m[1][1] + m[1][2] * m[1][2] + 0.3,
+            picked[18],
+        ] + [colour[:, ch * 128 : (ch + 1) * 128] for ch in range(3)]
+
+    for h in range(halves):
+        flat_out = rec_out[h].reshape(devices * rec_out[h].shape[1], 128)
+        for p, record in enumerate(records_of(h)):
+            flat_out[pl.ds(p, devices, stride=rec_out[h].shape[1]), :] = record
+        to_all(rec_out[h], rec_in[h], RECORDS, 2 + h)
+        rec_in[h][me] = rec_out[h][me]
+
+    tint_back[...] = jnp.concatenate([basis_parts[0], basis_parts[1], basis_parts[0]], axis=0)
     spans = [
         widen(basis_lanes + kind * 128, basis_lanes + (kind + 1) * 128) * hot for kind in range(5)
     ]
@@ -578,6 +605,10 @@
 
     for n in range(6, 12):
         fetches[n].wait()
+    high, low = split2(second_ref[...])
+    second_k[...] = jnp.concatenate([high, high, low], axis=1)
+    high, low = split2(across_ref[...])
+    across_k[...] = jnp.concatenate([high, high, low], axis=0)
     edges_wait(thalo_out, thalo_in, 0)
     in_rows, mid_rows = up8(rows + 2 * REACH), up8(rows + REACH)
     high_rows = 3 * mid_rows
@@ -604,65 +635,68 @@
     )
     mean_y, square_y = smooth([ext_y, ext_y * ext_y])
 
-    wait_all(geo_in, geo_rows, 2)
-    for k in range(TILE_MOST):
-        for t in range(tiles):
-            geo_pick[k, pl.ds(t, geo_rows, stride=tiles), :] = geo_in[
-                owners[k * tiles + t], 0:geo_rows, :
+    tile_row = lax.broadcasted_iota(jnp.int32, (tiles, pair_len), 0).astype(F32)
+    column = lax.rem(lanes_of((128, cols)), TILE).astype(F32) + (0.5 - 0.5 * TILE)
+
+    def prepare(h):
+        for k in range(TILE_MOST):
+            for t in range(tiles):
+                rec_pick[h, k, pl.ds(t, RECORDS, stride=tiles), :] = rec_in[h][
+                    owners[k * tiles + t], 0:RECORDS, :
+                ]
+
+        def gathered(p):
+            return jnp.concatenate(
+                [rec_pick[h, k, p * tiles : (p + 1) * tiles, :] for k in range(TILE_MOST)], axis=1
+            )
+
+        u_rel = gathered(0) - (tile_row * TILE + 0.5 * TILE)
+        w_rel = gathered(1) - ((band * rows).astype(F32) + 0.5 * TILE)
+        c_a, c_b, c_c, opac = [gathered(p) for p in range(2, GEO_REC)]
+        inv_det = 1.0 / (c_a * c_c - c_b * c_b)
+        coef_a = -0.5 * c_c * inv_det
+        coef_b = c_b * inv_det
+        coef_c = -0.5 * c_a * inv_det
+
+        def masked(value, other=0.0):
+            return jnp.where(keep, value, other)
+
+        quads = jnp.concatenate(
+            [
+                masked(LOG2_E * jnp.log(opac), NEVER),
+                LOG2_E * coef_a,
+                LOG2_E * coef_b,
+                LOG2_E * coef_c,
+                u_rel,
+                w_rel,
+            ],
+            axis=0,
+        )
+        tones = jnp.concatenate(
+            [masked(gathered(GEO_REC + ch)) for ch in range(3)], axis=0
+        )
+        grown = [
+            mx(stack3(quads), quad_ref[...], TN),
+            mx(stack3(tones), tone_ref[...], TN),
+        ]
+        for k in range(TILE_MOST):
+            at = k * block_len + h * 128
+            flat, part_a, part_b, part_c, u_wide, w_wide = [
+                grown[0][k * 128 : (k + 1) * 128, n * cols : (n + 1) * cols] for n in range(6)
             ]
-
-    def gathered(landed, p):
-        return jnp.concatenate(
-            [
-                landed[k, (p * halves + h) * tiles : (p * halves + h + 1) * tiles, :]
-                for k in range(TILE_MOST)
-                for h in range(halves)
-            ],
-            axis=1,
-        )
-
-    tile_row = lax.broadcasted_iota(jnp.int32, (tiles, window), 0).astype(F32)
-    u_rel = gathered(geo_pick, 0) - (tile_row * TILE + 0.5 * TILE)
-    w_rel = gathered(geo_pick, 1) - ((band * rows).astype(F32) + 0.5 * TILE)
-    c_a = gathered(geo_pick, 2)
-    c_b = gathered(geo_pick, 3)
-    c_c = gathered(geo_pick, 4)
-    opac = gathered(geo_pick, 5)
-    inv_det = 1.0 / (c_a * c_c - c_b * c_b)
-    coef_a = -0.5 * c_c * inv_det
-    coef_b = c_b * inv_det
-    coef_c = -0.5 * c_a * inv_det
-
-    def masked(value, other=0.0):
-        return jnp.where(keep, value, other)
-
-    flat = LOG2_E * (
-        coef_a * u_rel * u_rel + coef_b * u_rel * w_rel + coef_c * w_rel * w_rel
-    ) + LOG2_E * jnp.log(opac)
-    quads = jnp.concatenate(
-        [
-            masked(flat, NEVER),
-            masked(LOG2_E * (-2.0 * coef_a * u_rel - coef_b * w_rel)),
-            masked(LOG2_E * coef_a),
-            masked(LOG2_E * (-coef_b * u_rel - 2.0 * coef_c * w_rel)),
-            masked(LOG2_E * coef_b),
-            masked(LOG2_E * coef_c),
-        ],
-        axis=0,
-    )
-    grown = mx(stack3(quads), quad_ref[...], TN)
-    for n in range(3):
-        coef[n] = grown[:, n * cols : (n + 1) * cols]
-    wait_all(tint_in, tint_rows, 3)
-    for k in range(TILE_MOST):
-        for t in range(tiles):
-            tint_pick[k, pl.ds(t, tint_rows, stride=tiles), :] = tint_in[
-                owners[k * tiles + t], 0:tint_rows, :
-            ]
-    tones = jnp.concatenate([masked(gathered(tint_pick, ch)) for ch in range(3)], axis=0)
-    grown = mx(stack2(tones), tone_ref[...], TN)
-    for ch in range(3):
-        coef[3 + ch] = grown[:, ch * cols : (ch + 1) * cols]
+            e_x = column - u_wide
+            coef[0, at : at + 128, :] = flat + part_a * e_x * e_x
+            coef[1, at : at + 128, :] = part_b * e_x
+            coef[2, at : at + 128, :] = part_c
+            coef[6, at : at + 128, :] = w_wide
+            for ch in range(3):
+                coef[3 + ch, at : at + 128, :] = grown[1][
+                    k * 128 : (k + 1) * 128, ch * cols : (ch + 1) * cols
+                ]
+        return u_rel, w_rel, c_a, c_b, c_c, opac, inv_det, coef_a, coef_b, coef_c
+
+    wait_all(rec_in[0], RECORDS, 2)
+    shapes = [prepare(0)]
 
     sub8 = lax.broadcasted_iota(jnp.int32, (8, cols), 0).astype(F32)
     parts_n = rows // 8
@@ -677,10 +711,11 @@
         for k in range(8):
             j = group * 8 + k
             q0, q1, q2 = spread_row(0, j), spread_row(1, j), spread_row(2, j)
+            low = spread_row(6, j)
             tint = [spread_row(3 + ch, j) for ch in range(3)]
             for part in range(parts_n):
-                r = row_local[part]
-                alpha = jnp.exp2(q0 + r * (q1 + r * q2))
+                e_y = row_local[part] - low
+                alpha = jnp.exp2(q0 + e_y * (q1 + e_y * q2))
                 weight = alpha * trans[part]
                 alpha_s[j, part] = alpha
                 weight_s[j, part] = weight
@@ -691,12 +726,12 @@
         return tuple(trans), tuple(image)
 
     zero = jnp.zeros((8, cols), F32)
-    _, image = lax.fori_loop(
-        0,
-        window // 8,
-        blend,
-        (tuple([zero + 1.0] * parts_n), tuple([zero] * (3 * parts_n))),
-    )
+    state = (tuple([zero + 1.0] * parts_n), tuple([zero] * (3 * parts_n)))
+    state = lax.fori_loop(0, 128 // 8, blend, state, unroll=UNROLL)
+    for h in range(1, halves):
+        wait_all(rec_in[h], RECORDS, 2 + h)
+        shapes.append(prepare(h))
+    _, image = lax.fori_loop(128 // 8, window // 8, blend, state, unroll=UNROLL)
     pred = [
         jnp.concatenate([image[ch * parts_n + part] for part in range(parts_n)], axis=0)
         for ch in range(3)
@@ -734,11 +769,11 @@
         ],
         axis=1,
     )
-    down2 = jnp.dot(second_ref[...], adjoint, precision=HIGHEST_MODE, preferred_element_type=F32)
+    high, low = split2(adjoint)
+    down2 = mx(second_k[...], jnp.concatenate([high, low, high], axis=0))
     stacked2 = jnp.concatenate([down2[:, f * cols : (f + 1) * cols] for f in range(3)], axis=0)
-    spread = jnp.dot(
-        stacked2, across_ref[...], precision=HIGHEST_MODE, preferred_element_type=F32
-    )
+    high, low = split2(stacked2)
+    spread = mx(jnp.concatenate([high, low, high], axis=1), across_k[...])
     deep = 3 * rows
     pred_all = jnp.concatenate(pred, axis=0)
     mine_all = jnp.concatenate([mine[ch] for ch in range(3)], axis=0)
@@ -775,18 +810,20 @@
             moment_s[3 + ch, pl.ds(at, 8), :] = tree_sum(sums[ch], cols)
         return carry
 
-    lax.fori_loop(0, window // 8, shades, 0)
-
-    def route(value):
+    lax.fori_loop(0, window // 8, shades, 0, unroll=UNROLL)
+
+    def route(value, length):
         stack = jnp.concatenate(
-            [value[:, k * block_len : (k + 1) * block_len] for k in range(TILE_MOST)], axis=0
+            [value[:, k * length : (k + 1) * length] for k in range(TILE_MOST)], axis=0
         )
         return mx(put, stack2(stack))
 
     power = power_ref[...]
+    power_low = power[0:tiles].astype(BF16)
     shade_flat = shade_out.reshape(devices * shade_out.shape[1], 128)
     for ch in range(3):
-        routed = route(exact_dot(power[0:tiles], moment_s[3 + ch], NT))
+        high, low = split2(moment_s[3 + ch])
+        routed = route(mx(power_low, high, NT) + mx(power_low, low, NT), block_len)
         for h in range(halves):
             shade_flat[pl.ds(ch * halves + h, devices, stride=shade_out.shape[1]), :] = routed[
                 :, h * 128 : (h + 1) * 128
@@ -794,7 +831,7 @@
     shade_flat[pl.ds(tint_rows, devices, stride=shade_out.shape[1]), :] = jnp.broadcast_to(
         loss, (devices, 128)
     )
-    to_all(shade_out, shade_in, tint_rows + 1, 4)
+    to_all(shade_out, shade_in, tint_rows + 1, 2 + halves)
     shade_in[me] = shade_out[me]
 
     def unblend(step, behind):
@@ -811,7 +848,7 @@
                     tint[0] * pull[0][part] + tint[1] * pull[1][part] + tint[2] * pull[2][part]
                 )
                 gap = shade - behind[part]
-                behind[part] = alpha * shade + (1.0 - alpha) * behind[part]
+                behind[part] = behind[part] + alpha * gap
                 lean = weight_s[j, part] * gap
                 lean_r = lean * row_local[part]
                 terms = [lean, lean_r, lean_r * row_local[part]]
@@ -826,40 +863,52 @@
             moment_s[kind, pl.ds(at, 8), :] = tree_sum(sums[kind], cols)
         return tuple(behind)
 
-    lax.fori_loop(0, window // 8, unblend, tuple([zero] * parts_n))
-
-    by_x = exact_dot(power, moment_s[0], NT)
-    m_00, m_10, m_20 = by_x[0:tiles], by_x[tiles : 2 * tiles], by_x[2 * tiles : 3 * tiles]
-    by_xr = exact_dot(power[0 : 2 * tiles], moment_s[1], NT)
-    m_01, m_11 = by_xr[0:tiles], by_xr[tiles : 2 * tiles]
-    m_02 = exact_dot(power[0:tiles], moment_s[2], NT)
-    s_x = m_10 - u_rel * m_00
-    s_y = m_01 - w_rel * m_00
-    s_xx = m_20 - 2.0 * u_rel * m_10 + u_rel * u_rel * m_00
-    s_xy = m_11 - u_rel * m_01 - w_rel * m_10 + u_rel * w_rel * m_00
-    s_yy = m_02 - 2.0 * w_rel * m_01 + w_rel * w_rel * m_00
-    by_det = -(coef_a * s_xx + coef_b * s_xy + coef_c * s_yy) * inv_det
-    derivs = [
-        -(2.0 * coef_a * s_x + coef_b * s_y),
-        -(2.0 * coef_c * s_y + coef_b * s_x),
-        -0.5 * inv_det * s_yy + by_det * c_c,
-        inv_det * s_xy - 2.0 * c_b * by_det,
-        -0.5 * inv_det * s_xx + by_det * c_a,
-        m_00 / opac,
-    ]
-    grad_flat = grad_out.reshape(devices * grad_out.shape[1], 128)
-    for p in range(GEO_REC):
-        routed = route(derivs[p])
-        for h in range(halves):
-            grad_flat[pl.ds(p * halves + h, devices, stride=grad_out.shape[1]), :] = routed[
-                :, h * 128 : (h + 1) * 128
-            ]
-    to_all(grad_out, grad_in, geo_rows, 5)
-    grad_in[me] = grad_out[me]
-
-    wait_all(shade_in, tint_rows + 1, 4)
+    def derive(h):
+        u_rel, w_rel, c_a, c_b, c_c, opac, inv_det, coef_a, coef_b, coef_c = shapes[h]
+        moments = [
+            jnp.concatenate(
+                [
+                    moment_s[n, k * block_len + h * 128 : k * block_len + (h + 1) * 128, :]
+                    for k in range(TILE_MOST)
+                ],
+                axis=0,
+            )
+            for n in range(3)
+        ]
+        by_x = exact_dot(power, moments[0], NT)
+        m_00, m_10, m_20 = by_x[0:tiles], by_x[tiles : 2 * tiles], by_x[2 * tiles : 3 * tiles]
+        by_xr = exact_dot(power[0 : 2 * tiles], moments[1], NT)
+        m_01, m_11 = by_xr[0:tiles], by_xr[tiles : 2 * tiles]
+        m_02 = exact_dot(power[0:tiles], moments[2], NT)
+        s_x = m_10 - u_rel * m_00
+        s_y = m_01 - w_rel * m_00
+        s_xx = m_20 - 2.0 * u_rel * m_10 + u_rel * u_rel * m_00
+        s_xy = m_11 - u_rel * m_01 - w_rel * m_10 + u_rel * w_rel * m_00
+        s_yy = m_02 - 2.0 * w_rel * m_01 + w_rel * w_rel * m_00
+        by_det = -(coef_a * s_xx + coef_b * s_xy + coef_c * s_yy) * inv_det
+        derivs = [
+            -(2.0 * coef_a * s_x + coef_b * s_y),
+            -(2.0 * coef_c * s_y + coef_b * s_x),
+            -0.5 * inv_det * s_yy + by_det * c_c,
+            inv_det * s_xy - 2.0 * c_b * by_det,
+            -0.5 * inv_det * s_xx + by_det * c_a,
+            m_00 / opac,
+        ]
+        flat_out = grad_out[h].reshape(devices * grad_out[h].shape[1], 128)
+        for p in range(GEO_REC):
+            flat_out[pl.ds(p, devices, stride=grad_out[h].shape[1]), :] = route(derivs[p], 128)
+        to_all(grad_out[h], grad_in[h], GEO_REC, 2 + halves + 1 + h)
+        grad_in[h][me] = grad_out[h][me]
+
+    groups = window // 8
+    last = groups - 128 // 8
+    behind = lax.fori_loop(0, last, unblend, tuple([zero] * parts_n), unroll=UNROLL)
+    for h in range(halves - 1, 0, -1):
+        derive(h)
+    lax.fori_loop(last, groups, unblend, behind, unroll=UNROLL)
+    derive(0)
+    wait_all(shade_in, tint_rows + 1, 2 + halves)
     shade_back = shade_in.reshape(devices * shade_in.shape[1], 128)
-    grad_back = grad_in.reshape(devices * grad_in.shape[1], 128)
 
     def arrived(landed, stride, p):
         return jnp.concatenate(
@@ -882,8 +931,23 @@
     fetches[12].wait()
     fetches[13].wait()
 
-    wait_all(grad_in, geo_rows, 5)
-    geos = [arrived(grad_back, grad_in.shape[1], p) for p in range(GEO_REC)]
+    def update(c, carry):
+        adam_step(c, grad_ref, (gauss_ref, one_ref, two_ref), (gauss_ref, one_ref, two_ref))
+        return carry
+
+    lax.fori_loop(SHAPE_COMPS, gauss_ref.shape[0], update, 0, unroll=4)
+
+    for h in range(halves - 1, -1, -1):
+        wait_all(grad_in[h], GEO_REC, 2 + halves + 1 + h)
+    grad_back = [
+        grad_in[h].reshape(devices * grad_in[h].shape[1], 128) for h in range(halves)
+    ]
+    geos = [
+        jnp.concatenate(
+            [back[pl.ds(p, devices, stride=grad_in[0].shape[1]), :] for back in grad_back], axis=1
+        )
+        for p in range(GEO_REC)
+    ]
     line = spread_back(line_back, [geos[0], geos[1], geos[5]])
     shape = spread_back(shape_back, geos[2:5])
 
@@ -914,60 +978,36 @@
     two_v,
     write_sem,
 ):
-    whole = pltpu.make_async_copy(grad_ref, out_grad, write_sem.at[3, 0])
-    whole.start()
-    total = pltpu.make_async_copy(loss_in, loss_out, write_sem.at[3, 1])
-    total.start()
     comps = gauss_ref.shape[0]
-    pieces = [whole, total]
-    for piece in range(PIECES):
-        low, high = piece * comps // PIECES, (piece + 1) * comps // PIECES
-
-        def update(c, carry):
-            gradient = grad_ref[c]
-            new_one = 0.9 * one_ref[c] + 0.1 * gradient
-            new_two = 0.999 * two_ref[c] + 0.001 * gradient * gradient
-            one_v[c] = new_one
-            two_v[c] = new_two
-            bottom = jnp.sqrt(new_two * (1.0 / BIAS_SECOND)) + 1e-08
-            gauss_v[c] = gauss_ref[c] - learning_rate(c) * new_one / bottom
-            return carry
-
-        lax.fori_loop(low, high, update, 0, unroll=2)
+    held = [(grad_ref, out_grad), (gauss_ref, out_gauss), (one_ref, out_one), (two_ref, out_two)]
+    fresh = [(gauss_v, out_gauss), (one_v, out_one), (two_v, out_two)]
+    copies = [pltpu.make_async_copy(loss_in, loss_out, write_sem.at[4, 0])]
+    copies[0].start()
+
+    def send(group, low, high, slot):
         part = pl.ds(low, high - low)
-        for source, landing, sem in (
-            (one_v, out_one, 0),
-            (two_v, out_two, 1),
-            (gauss_v, out_gauss, 2),
-        ):
+        for n, (source, landing) in enumerate(group):
             copy = pltpu.make_async_copy(
-                source.at[part], landing.at[part], write_sem.at[sem, piece]
+                source.at[part], landing.at[part], write_sem.at[n, slot]
             )
             copy.start()
-            pieces.append(copy)
-    for copy in pieces:
+            copies.append(copy)
+
+    for piece in range(PIECES):
+        low = SHAPE_COMPS + piece * (comps - SHAPE_COMPS) // PIECES
+        high = SHAPE_COMPS + (piece + 1) * (comps - SHAPE_COMPS) // PIECES
+        send(held, low, high, piece)
+    send(held[0:1], 0, SHAPE_COMPS, PIECES)
+    for c in range(SHAPE_COMPS):
+        adam_step(c, grad_ref, (gauss_ref, one_ref, two_ref), (gauss_v, one_v, two_v))
+    send(fresh, 0, SHAPE_COMPS, PIECES + 1)
+    for copy in copies:
         copy.wait()
 
 
-def quad_table(tiles, cols):
-    lane = np.arange(cols)
-    local = lane % TILE + 0.5 - TILE / 2
-    belongs = (lane[None, :] // TILE == np.arange(tiles)[:, None]).astype(np.float32)
-    nothing = np.zeros_like(belongs)
-    rows = [
-        [belongs, nothing, nothing],
-        [belongs * local, nothing, nothing],
-        [belongs * local * local, nothing, nothing],
-        [nothing, belongs, nothing],
-        [nothing, belongs * local, nothing],
-        [nothing, nothing, belongs],
-    ]
-    return np.tile(np.block(rows), (3, 1))
-
-
-def tone_table(tiles, cols):
+def wide_table(tiles, cols, kinds):
     belongs = (np.arange(cols)[None, :] // TILE == np.arange(tiles)[:, None]).astype(np.float32)
-    return np.tile(np.kron(np.eye(3, dtype=np.float32), belongs), (2, 1))
+    return np.tile(np.kron(np.eye(kinds, dtype=np.float32), belongs), (3, 1))
 
 
 def per_device(
@@ -993,8 +1033,8 @@
 
     across, first, second = smoothing_tables(rows, cols, 3)
     power = power_table(tiles, cols)
-    quad = quad_table(tiles, cols).astype(BF16)
-    tone = tone_table(tiles, cols).astype(BF16)
+    quad = wide_table(tiles, cols, 6).astype(BF16)
+    tone = wide_table(tiles, cols, 3).astype(BF16)
     vmem = pl.BlockSpec(memory_space=pltpu.VMEM)
     hbm = pl.BlockSpec(memory_space=pltpu.HBM)
 
@@ -1002,7 +1042,7 @@
         return jnp.transpose(array, (1, 0, 2))
 
     window = TILE_MOST * block_len
-    geo_pad, tint_pad = up8(GEO_REC * halves), up8(3 * halves + 1)
+    tint_pad = up8(3 * halves + 1)
     basis_lanes = BASIS * blocks
     shape = jax.ShapeDtypeStruct((comps, blocks, block_len), F32)
     scalar = jax.ShapeDtypeStruct((1, 1), F32)
@@ -1021,38 +1061,38 @@
             pltpu.VMEM(across.shape, F32),
             pltpu.VMEM(first.shape, F32),
             pltpu.VMEM(second.shape, F32),
+            pltpu.VMEM((second.shape[0], 3 * second.shape[1]), BF16),
+            pltpu.VMEM((3 * cols, cols), BF16),
             pltpu.VMEM(power.shape, F32),
             pltpu.VMEM(quad.shape, BF16),
             pltpu.VMEM(tone.shape, BF16),
             pltpu.VMEM((views_n, 1, 128), F32),
             pltpu.VMEM((devices, 1, 128), F32),
+            pltpu.VMEM((devices, 128), F32),
             pltpu.VMEM((128, 128), BF16),
             pltpu.VMEM((128, basis_lanes + 5 * 128), BF16),
-            pltpu.VMEM((GEO_COMPS, 3 * blocks, block_len), BF16),
-            pltpu.VMEM((3, 2, basis_lanes, block_len), BF16),
+            pltpu.VMEM((halves, GEO_COMPS, 3 * blocks, 128), BF16),
+            pltpu.VMEM((halves, 3, basis_lanes, 3 * 128), BF16),
             pltpu.VMEM((3 * devices, basis_lanes), BF16),
             pltpu.VMEM((9 * devices, 128), BF16),
             pltpu.VMEM((9 * devices, 128), BF16),
-            pltpu.VMEM((devices, geo_pad, 128), F32),
-            pltpu.VMEM((devices, geo_pad, 128), F32),
+            (pltpu.VMEM((devices, up8(RECORDS), 128), F32),) * halves,
+            (pltpu.VMEM((devices, up8(RECORDS), 128), F32),) * halves,
+            pltpu.VMEM((halves, TILE_MOST, RECORDS * tiles, 128), F32),
             pltpu.VMEM((devices, tint_pad, 128), F32),
             pltpu.VMEM((devices, tint_pad, 128), F32),
-            pltpu.VMEM((TILE_MOST, GEO_REC * halves * tiles, 128), F32),
-            pltpu.VMEM((TILE_MOST, 3 * halves * tiles, 128), F32),
-            pltpu.VMEM((devices, tint_pad, 128), F32),
-            pltpu.VMEM((devices, tint_pad, 128), F32),
-            pltpu.VMEM((devices, geo_pad, 128), F32),
-            pltpu.VMEM((devices, geo_pad, 128), F32),
+            (pltpu.VMEM((devices, up8(GEO_REC), 128), F32),) * halves,
+            (pltpu.VMEM((devices, up8(GEO_REC), 128), F32),) * halves,
             pltpu.VMEM((2, 3, REACH, cols), F32),
             pltpu.VMEM((2, 3, REACH, cols), F32),
             pltpu.VMEM((2, 3, REACH, cols), F32),
             pltpu.VMEM((2, 3, REACH, cols), F32),
-            pltpu.VMEM((6, window, cols), F32),
+            pltpu.VMEM((7, window, cols), F32),
             pltpu.VMEM((window, rows // 8, 8, cols), F32),
             pltpu.VMEM((window, rows // 8, 8, cols), F32),
             pltpu.VMEM((6, window, cols), F32),
-            pltpu.SemaphoreType.DMA((6,)),
-            pltpu.SemaphoreType.DMA((6,)),
+            pltpu.SemaphoreType.DMA((3 + 2 * halves,)),
+            pltpu.SemaphoreType.DMA((3 + 2 * halves,)),
             pltpu.SemaphoreType.DMA((2, 2)),
             pltpu.SemaphoreType.DMA((2, 2)),
             pltpu.SemaphoreType.DMA((14,)),
@@ -1088,8 +1128,8 @@
         out_shape=(shape, shape, shape, shape, scalar),
         in_specs=[vmem] * 5,
         out_specs=(hbm, hbm, hbm, hbm, hbm),
-        scratch_shapes=[pltpu.VMEM((comps, blocks, block_len), F32)] * 3
-        + [pltpu.SemaphoreType.DMA((4, PIECES))],
+        scratch_shapes=[pltpu.VMEM((SHAPE_COMPS, blocks, block_len), F32)] * 3
+        + [pltpu.SemaphoreType.DMA((5, PIECES + 2))],
         compiler_params=pltpu.CompilerParams(vmem_limit_bytes=16 * 1024 * 1024),
         name="adam_step",
     )(gradient, params, one, two, mean_loss)

time: 46.3 us -> 43 us (0.929)
  Pallas kernels: 45.5 us -> 42.2 us
    pallas_call x1, Pallas kernels: 42.7 us -> 39.4 us  [per_device(): pl.pallas_call(functools.partial(step_kernel, geometry), out_shape=(kept,...]
where the time goes in v2:
time: 43 us; the launch traced here: 42.8 us
  Pallas kernels  42.2 us (98%)
  between operations  0.64 us (1%)
    pallas_call x1, Pallas kernels, per_device(): pl.pallas_call(functools.partial(step_kernel, geometry), out_shape=(kept,...  39.4 us
    pallas_call x1, Pallas kernels, per_device(): pl.pallas_call(adam_kernel, out_shape=(shape, shape, shape, shape, scalar...  2.8 us

profile of v2, /device:TPU:0, one launch (start us, length us, event | category | flops | bytes accessed | tf_op | source)
XLA Modules:
  0.0 42.8 jit_solution(16775736834389573463)
XLA Ops:
  0.6 39.4 %render_step.1 = (f32[62,16,256]{2,1,0:T(8,128)S(1)}, f32[62,16,256]{2,1,0:T(8,128)S(1)}, f32[62,16,256]{2,1,0:T(8,128)S(1)}, f32[62,16,256]{2,1,0:T(8,128)S(1)}, f32[1,1]{1,0:T(1,128)}) custom-call(f32[1,9]{1,0:T(1,128)} %camera_hbm.1, s32[1,1,16]{2,1,0:T(1,128)} %list_hbm.1, s32[1,1,8]{2,1,0:T(1,128)} %start_hbm.1, s32[1,1,8]{2,1,0:T(1,128)} %end_hbm.1, ...), custom_call_target="tpu_custom_call" | custom-call | tf_op jit(solution)/shard_map/render_step/pallas_call | solution.py:1050
  40.0 2.8 %adam_step.1 = (f32[62,16,256]{2,1,0:T(8,128)}, f32[62,16,256]{2,1,0:T(8,128)}, f32[62,16,256]{2,1,0:T(8,128)}, f32[62,16,256]{2,1,0:T(8,128)}, f32[1,1]{1,0:T(1,128)}) custom-call(f32[62,16,256]{2,1,0:T(8,128)S(1)} %get-tuple-element.15.grad_ref, f32[62,16,256]{2,1,0:T(8,128)S(1)} %get-tuple-element.16.gauss_ref, ...), custom_call_target="tpu_custom_call" | custom-call | tf_op jit(solution)/shard_map/adam_step/pallas_call | solution.py:1126

commit v3 on v2

--- a/solution.py
+++ b/solution.py
@@ -168,27 +168,6 @@
         term = mx(table, part, dims)
         total = term if total is None else total + term
     return total
-
-
-def tree_sum(vregs, lane_count):
-    sub = lax.broadcasted_iota(jnp.int32, (8, lane_count), 0)
-
-    def join(a, b, mask, shift):
-        return jnp.where(mask, a, b) + pltpu.roll(jnp.where(mask, b, a), 8 - shift, 0)
-
-    def half(offset):
-        return ((sub + (8 - offset)) % 8) < 4
-
-    def quarter(offset):
-        return ((sub + (8 - offset)) % 4) < 2
-
-    z1 = join(
-        join(vregs[0], vregs[4], half(0), 4), join(vregs[2], vregs[6], half(2), 4), quarter(0), 2
-    )
-    z2 = join(
-        join(vregs[1], vregs[5], half(1), 4), join(vregs[3], vregs[7], half(3), 4), quarter(1), 2
-    )
-    return join(z1, z2, (sub % 2) < 1, 1)
 
 
 def adam_step(c, grad_ref, source, landing):
@@ -281,6 +260,7 @@
     msg_out,
     msg_in,
     asked_ref,
+    loss_v,
     hot_map,
     wide_map,
     geo_tab,
@@ -795,8 +775,20 @@
         for ch in range(3)
     ]
 
+    upper = lax.broadcasted_iota(jnp.int32, (8, cols), 0) < 4
+
+    def keep_pair(held, kind, group, k, total):
+        other = held.pop((kind, k // 2), None)
+        if other is None:
+            held[kind, k // 2] = total
+            return
+        a, b = (other, total) if k % 2 else (total, other)
+        joined = jnp.where(upper, a, b) + pltpu.roll(jnp.where(upper, b, a), 4, 0)
+        at = pl.multiple_of(group * 32 + k // 2 * 8, 8)
+        moment_s[kind, pl.ds(at, 8), :] = joined
+
     def shades(group, carry):
-        sums = [[None] * 8 for _ in range(3)]
+        held = {}
         for k in range(8):
             j = group * 8 + k
             weight = [weight_s[j, part] for part in range(parts_n)]
@@ -804,11 +796,13 @@
                 total = weight[0] * pull[ch][0]
                 for part in range(1, parts_n):
                     total = total + weight[part] * pull[ch][part]
-                sums[ch][k] = total
-        at = pl.multiple_of(group * 8, 8)
-        for ch in range(3):
-            moment_s[3 + ch, pl.ds(at, 8), :] = tree_sum(sums[ch], cols)
+                keep_pair(held, ch, group, k, total)
         return carry
+
+    def summed(kind, start, count):
+        folded = moment_s.at[kind]
+        quarter = [folded[pl.ds(start * 4 + sub, count, stride=4), :] for sub in range(4)]
+        return (quarter[0] + quarter[1]) + (quarter[2] + quarter[3])
 
     lax.fori_loop(0, window // 8, shades, 0, unroll=UNROLL)
 
@@ -822,7 +816,7 @@
     power_low = power[0:tiles].astype(BF16)
     shade_flat = shade_out.reshape(devices * shade_out.shape[1], 128)
     for ch in range(3):
-        high, low = split2(moment_s[3 + ch])
+        high, low = split2(summed(ch, 0, window))
         routed = route(mx(power_low, high, NT) + mx(power_low, low, NT), block_len)
         for h in range(halves):
             shade_flat[pl.ds(ch * halves + h, devices, stride=shade_out.shape[1]), :] = routed[
@@ -837,7 +831,7 @@
     def unblend(step, behind):
         group = window // 8 - 1 - step
         behind = list(behind)
-        sums = [[None] * 8 for _ in range(3)]
+        held = {}
         for k in reversed(range(8)):
             j = group * 8 + k
             tint = [spread_row(3 + ch, j) for ch in range(3)]
@@ -857,20 +851,14 @@
                     for value, total in zip(terms, totals)
                 ]
             for kind in range(3):
-                sums[kind][k] = totals[kind]
-        at = pl.multiple_of(group * 8, 8)
-        for kind in range(3):
-            moment_s[kind, pl.ds(at, 8), :] = tree_sum(sums[kind], cols)
+                keep_pair(held, kind, group, k, totals[kind])
         return tuple(behind)
 
     def derive(h):
         u_rel, w_rel, c_a, c_b, c_c, opac, inv_det, coef_a, coef_b, coef_c = shapes[h]
         moments = [
             jnp.concatenate(
-                [
-                    moment_s[n, k * block_len + h * 128 : k * block_len + (h + 1) * 128, :]
-                    for k in range(TILE_MOST)
-                ],
+                [summed(n, k * block_len + h * 128, 128) for k in range(TILE_MOST)],
                 axis=0,
             )
             for n in range(3)
@@ -925,9 +913,11 @@
         for q in range(BASIS):
             grad_ref[14 + 3 * q + ch] = colour[q * blocks : (q + 1) * blocks]
     losses = shade_back[pl.ds(tint_rows, devices, stride=shade_in.shape[1]), :]
-    loss_ref[...] = jnp.sum(losses, axis=0, keepdims=True)[:, 0:1] * (
+    loss_v[...] = jnp.sum(losses, axis=0, keepdims=True)[:, 0:1] * (
         1.0 / (devices * rows * cols)
     )
+    loss_copy = pltpu.make_async_copy(loss_v, loss_ref, fetch_sem.at[len(sources)])
+    loss_copy.start()
     fetches[12].wait()
     fetches[13].wait()
 
@@ -960,6 +950,7 @@
     columns = [comp(line, n) for n in range(TERM_ROWS)] + list(d_logs) + list(d_quats) + [d_logit]
     for c, value in enumerate(columns):
         grad_ref[c] = value
+    loss_copy.wait()
 
 
 def adam_kernel(
@@ -1049,9 +1040,9 @@
     kept = pltpu.VMEM(shape.shape, F32)
     gradient, params, one, two, mean_loss = pl.pallas_call(
         functools.partial(step_kernel, geometry),
-        out_shape=(kept, kept, kept, kept, pltpu.VMEM((1, 1), F32)),
+        out_shape=(kept, kept, kept, kept, pltpu.HBM((1, 1), F32)),
         in_specs=[hbm] * 14,
-        out_specs=(vmem,) * 5,
+        out_specs=(vmem,) * 4 + (hbm,),
         scratch_shapes=[
             pltpu.SMEM((1, 9), F32),
             pltpu.SMEM((1, 1, list_len), jnp.int32),
@@ -1069,6 +1060,7 @@
             pltpu.VMEM((views_n, 1, 128), F32),
             pltpu.VMEM((devices, 1, 128), F32),
             pltpu.VMEM((devices, 128), F32),
+            pltpu.VMEM((1, 1), F32),
             pltpu.VMEM((128, 128), BF16),
             pltpu.VMEM((128, basis_lanes + 5 * 128), BF16),
             pltpu.VMEM((halves, GEO_COMPS, 3 * blocks, 128), BF16),
@@ -1090,12 +1082,12 @@
             pltpu.VMEM((7, window, cols), F32),
             pltpu.VMEM((window, rows // 8, 8, cols), F32),
             pltpu.VMEM((window, rows // 8, 8, cols), F32),
-            pltpu.VMEM((6, window, cols), F32),
+            pltpu.VMEM((3, window * 4, cols), F32),
             pltpu.SemaphoreType.DMA((3 + 2 * halves,)),
             pltpu.SemaphoreType.DMA((3 + 2 * halves,)),
             pltpu.SemaphoreType.DMA((2, 2)),
             pltpu.SemaphoreType.DMA((2, 2)),
-            pltpu.SemaphoreType.DMA((14,)),
+            pltpu.SemaphoreType.DMA((15,)),
         ],
         compiler_params=pltpu.CompilerParams(
             collective_id=0, has_side_effects=True, vmem_limit_bytes=40 * 1024 * 1024
@@ -1126,13 +1118,13 @@
     new_params, new_one, new_two, out_gradient, out_loss = pl.pallas_call(
         adam_kernel,
         out_shape=(shape, shape, shape, shape, scalar),
-        in_specs=[vmem] * 5,
+        in_specs=[vmem] * 4 + [hbm],
         out_specs=(hbm, hbm, hbm, hbm, hbm),
         scratch_shapes=[pltpu.VMEM((SHAPE_COMPS, blocks, block_len), F32)] * 3
         + [pltpu.SemaphoreType.DMA((5, PIECES + 2))],
         compiler_params=pltpu.CompilerParams(vmem_limit_bytes=16 * 1024 * 1024),
         name="adam_step",
-    )(gradient, params, one, two, mean_loss)
+    )(gradient, params, one, two, pltpu.with_memory_space_constraint(mean_loss, pltpu.HBM))
     return (
         by_comp(new_params),
         by_comp(new_one),

time: 43 us -> 42.2 us (0.981)
  Pallas kernels: 42.2 us -> 41.4 us
    pallas_call x1, Pallas kernels: 39.4 us -> 38.6 us  [per_device(): pl.pallas_call(functools.partial(step_kernel, geometry), out_shape=(kept,...]
where the time goes in v3:
time: 42.2 us; the launch traced here: 42.1 us
  Pallas kernels  41.4 us (98%)
  between operations  0.64 us (2%)
    pallas_call x1, Pallas kernels, per_device(): pl.pallas_call(functools.partial(step_kernel, geometry), out_shape=(kept,...  38.6 us
    pallas_call x1, Pallas kernels, per_device(): pl.pallas_call(adam_kernel, out_shape=(shape, shape, shape, shape, scalar...  2.8 us

profile of v3, /device:TPU:0, one launch (start us, length us, event | category | flops | bytes accessed | tf_op | source)
XLA Modules:
  0.0 42.1 jit_solution(18133493904554120955)
XLA Ops:
  0.6 38.6 %render_step.1 = (f32[62,16,256]{2,1,0:T(8,128)S(1)}, f32[62,16,256]{2,1,0:T(8,128)S(1)}, f32[62,16,256]{2,1,0:T(8,128)S(1)}, f32[62,16,256]{2,1,0:T(8,128)S(1)}, f32[1,1]{1,0:T(1,128)}) custom-call(f32[1,9]{1,0:T(1,128)} %camera_hbm.1, s32[1,1,16]{2,1,0:T(1,128)} %list_hbm.1, s32[1,1,8]{2,1,0:T(1,128)} %start_hbm.1, s32[1,1,8]{2,1,0:T(1,128)} %end_hbm.1, ...), custom_call_target="tpu_custom_call" | custom-call | tf_op jit(solution)/shard_map/render_step/pallas_call | solution.py:1041
  39.3 2.8 %adam_step.1 = (f32[62,16,256]{2,1,0:T(8,128)}, f32[62,16,256]{2,1,0:T(8,128)}, f32[62,16,256]{2,1,0:T(8,128)}, f32[62,16,256]{2,1,0:T(8,128)}, f32[1,1]{1,0:T(1,128)}) custom-call(f32[62,16,256]{2,1,0:T(8,128)S(1)} %get-tuple-element.15.grad_ref, f32[62,16,256]{2,1,0:T(8,128)S(1)} %get-tuple-element.16.gauss_ref, ...), custom_call_target="tpu_custom_call" | custom-call | tf_op jit(solution)/shard_map/adam_step/pallas_call | solution.py:1118

commit v4 on v3

--- a/solution.py
+++ b/solution.py
@@ -93,13 +93,6 @@
     return across, first, second
 
 
-def power_table(tiles, cols):
-    lane = np.arange(cols)
-    local = lane % TILE + 0.5 - TILE / 2
-    belongs = (lane[None, :] // TILE == np.arange(tiles)[:, None]).astype(np.float32)
-    return np.concatenate([belongs, belongs * local, belongs * local * local]).astype(np.float32)
-
-
 def harmonics(dir_x, dir_y, dir_z):
     sq_x, sq_y, sq_z = (dir_x * dir_x, dir_y * dir_y, dir_z * dir_z)
     return [
@@ -153,14 +146,6 @@
     return high, (value - high.astype(F32)).astype(BF16)
 
 
-def stack3(value):
-    return jnp.concatenate(split3(value), axis=0)
-
-
-def stack2(value):
-    return jnp.concatenate(split2(value), axis=0)
-
-
 def exact_dot(table, value, dims):
     table = table.astype(BF16)
     total = None
@@ -168,6 +153,14 @@
         term = mx(table, part, dims)
         total = term if total is None else total + term
     return total
+
+
+def stack3(value):
+    return jnp.concatenate(split3(value), axis=0)
+
+
+def stack2(value):
+    return jnp.concatenate(split2(value), axis=0)
 
 
 def adam_step(c, grad_ref, source, landing):
@@ -237,6 +230,7 @@
     first_hbm,
     second_hbm,
     power_hbm,
+    shade_hbm,
     quad_hbm,
     tone_hbm,
     grad_ref,
@@ -255,6 +249,7 @@
     second_k,
     across_k,
     power_ref,
+    shade_ref,
     quad_ref,
     tone_ref,
     msg_out,
@@ -325,6 +320,7 @@
         (quad_hbm, quad_ref),
         (tone_hbm, tone_ref),
         (power_hbm, power_ref),
+        (shade_hbm, shade_ref),
         (across_hbm, across_ref),
         (first_hbm, first_ref),
         (second_hbm, second_ref),
@@ -583,7 +579,7 @@
         high, low = split2(jnp.concatenate(group, axis=0))
         landing[...] = jnp.concatenate([high, low, high], axis=0)
 
-    for n in range(6, 12):
+    for n in range(6, 13):
         fetches[n].wait()
     high, low = split2(second_ref[...])
     second_k[...] = jnp.concatenate([high, high, low], axis=1)
@@ -812,12 +808,11 @@
         )
         return mx(put, stack2(stack))
 
-    power = power_ref[...]
-    power_low = power[0:tiles].astype(BF16)
     shade_flat = shade_out.reshape(devices * shade_out.shape[1], 128)
+    folded = [piece for ch in range(3) for piece in split2(summed(ch, 0, window))]
+    by_tile = jnp.transpose(mx(jnp.concatenate(folded, axis=1), shade_ref[...]))
     for ch in range(3):
-        high, low = split2(summed(ch, 0, window))
-        routed = route(mx(power_low, high, NT) + mx(power_low, low, NT), block_len)
+        routed = route(by_tile[ch * tiles : (ch + 1) * tiles], block_len)
         for h in range(halves):
             shade_flat[pl.ds(ch * halves + h, devices, stride=shade_out.shape[1]), :] = routed[
                 :, h * 128 : (h + 1) * 128
@@ -863,6 +858,7 @@
             )
             for n in range(3)
         ]
+        power = power_ref[...]
         by_x = exact_dot(power, moments[0], NT)
         m_00, m_10, m_20 = by_x[0:tiles], by_x[tiles : 2 * tiles], by_x[2 * tiles : 3 * tiles]
         by_xr = exact_dot(power[0 : 2 * tiles], moments[1], NT)
@@ -918,8 +914,8 @@
     )
     loss_copy = pltpu.make_async_copy(loss_v, loss_ref, fetch_sem.at[len(sources)])
     loss_copy.start()
-    fetches[12].wait()
     fetches[13].wait()
+    fetches[14].wait()
 
     def update(c, carry):
         adam_step(c, grad_ref, (gauss_ref, one_ref, two_ref), (gauss_ref, one_ref, two_ref))
@@ -972,28 +968,43 @@
     comps = gauss_ref.shape[0]
     held = [(grad_ref, out_grad), (gauss_ref, out_gauss), (one_ref, out_one), (two_ref, out_two)]
     fresh = [(gauss_v, out_gauss), (one_v, out_one), (two_v, out_two)]
-    copies = [pltpu.make_async_copy(loss_in, loss_out, write_sem.at[4, 0])]
-    copies[0].start()
-
-    def send(group, low, high, slot):
+    total = pltpu.make_async_copy(loss_in, loss_out, write_sem.at[4])
+    total.start()
+
+    def send(group, low, high, first):
         part = pl.ds(low, high - low)
-        for n, (source, landing) in enumerate(group):
+        for n, (source, landing) in enumerate(group, first):
             copy = pltpu.make_async_copy(
-                source.at[part], landing.at[part], write_sem.at[n, slot]
+                source.at[part], landing.at[part], write_sem.at[n]
             )
             copy.start()
-            copies.append(copy)
 
     for piece in range(PIECES):
         low = SHAPE_COMPS + piece * (comps - SHAPE_COMPS) // PIECES
         high = SHAPE_COMPS + (piece + 1) * (comps - SHAPE_COMPS) // PIECES
-        send(held, low, high, piece)
-    send(held[0:1], 0, SHAPE_COMPS, PIECES)
+        send(held, low, high, 0)
+    send(held[0:1], 0, SHAPE_COMPS, 0)
     for c in range(SHAPE_COMPS):
         adam_step(c, grad_ref, (gauss_ref, one_ref, two_ref), (gauss_v, one_v, two_v))
-    send(fresh, 0, SHAPE_COMPS, PIECES + 1)
-    for copy in copies:
-        copy.wait()
+    send(fresh, 0, SHAPE_COMPS, 1)
+    total.wait()
+    for n, (source, landing) in enumerate(held):
+        pltpu.make_async_copy(source, landing, write_sem.at[n]).wait()
+
+
+def power_table(tiles, cols):
+    lane = np.arange(cols)
+    local = lane % TILE + 0.5 - TILE / 2
+    belongs = (lane[None, :] // TILE == np.arange(tiles)[:, None]).astype(np.float32)
+    return np.concatenate([belongs, belongs * local, belongs * local * local]).astype(np.float32)
+
+
+def shade_table(tiles, cols):
+    belongs = (np.arange(cols)[:, None] // TILE == np.arange(tiles)[None, :]).astype(np.float32)
+    table = np.zeros((3, 2, cols, cols), np.float32)
+    for ch in range(3):
+        table[ch, :, :, ch * tiles : (ch + 1) * tiles] = belongs
+    return table.reshape(6 * cols, cols)
 
 
 def wide_table(tiles, cols, kinds):
@@ -1024,6 +1035,7 @@
 
     across, first, second = smoothing_tables(rows, cols, 3)
     power = power_table(tiles, cols)
+    shade = shade_table(tiles, cols).astype(BF16)
     quad = wide_table(tiles, cols, 6).astype(BF16)
     tone = wide_table(tiles, cols, 3).astype(BF16)
     vmem = pl.BlockSpec(memory_space=pltpu.VMEM)
@@ -1041,7 +1053,7 @@
     gradient, params, one, two, mean_loss = pl.pallas_call(
         functools.partial(step_kernel, geometry),
         out_shape=(kept, kept, kept, kept, pltpu.HBM((1, 1), F32)),
-        in_specs=[hbm] * 14,
+        in_specs=[hbm] * 15,
         out_specs=(vmem,) * 4 + (hbm,),
         scratch_shapes=[
             pltpu.SMEM((1, 9), F32),
@@ -1055,6 +1067,7 @@
             pltpu.VMEM((second.shape[0], 3 * second.shape[1]), BF16),
             pltpu.VMEM((3 * cols, cols), BF16),
             pltpu.VMEM(power.shape, F32),
+            pltpu.VMEM(shade.shape, BF16),
             pltpu.VMEM(quad.shape, BF16),
             pltpu.VMEM(tone.shape, BF16),
             pltpu.VMEM((views_n, 1, 128), F32),
@@ -1087,7 +1100,7 @@
             pltpu.SemaphoreType.DMA((3 + 2 * halves,)),
             pltpu.SemaphoreType.DMA((2, 2)),
             pltpu.SemaphoreType.DMA((2, 2)),
-            pltpu.SemaphoreType.DMA((15,)),
+            pltpu.SemaphoreType.DMA((16,)),
         ],
         compiler_params=pltpu.CompilerParams(
             collective_id=0, has_side_effects=True, vmem_limit_bytes=40 * 1024 * 1024
@@ -1109,6 +1122,7 @@
                 first,
                 second,
                 power,
+                shade,
                 quad,
                 tone,
             )
@@ -1121,7 +1135,7 @@
         in_specs=[vmem] * 4 + [hbm],
         out_specs=(hbm, hbm, hbm, hbm, hbm),
         scratch_shapes=[pltpu.VMEM((SHAPE_COMPS, blocks, block_len), F32)] * 3
-        + [pltpu.SemaphoreType.DMA((5, PIECES + 2))],
+        + [pltpu.SemaphoreType.DMA((5,))],
         compiler_params=pltpu.CompilerParams(vmem_limit_bytes=16 * 1024 * 1024),
         name="adam_step",
     )(gradient, params, one, two, pltpu.with_memory_space_constraint(mean_loss, pltpu.HBM))

time: 42.2 us -> 42 us (level)
  no operation moved by 1% of the time
where the time goes in v4:
time: 42 us; the launch traced here: 41.9 us
  Pallas kernels  41.2 us (98%)
  between operations  0.64 us (2%)
    pallas_call x1, Pallas kernels, per_device(): pl.pallas_call(functools.partial(step_kernel, geometry), out_shape=(kept,...  38.6 us
    pallas_call x1, Pallas kernels, per_device(): pl.pallas_call(adam_kernel, out_shape=(shape, shape, shape, shape, scalar...  2.62 us

profile of v4, /device:TPU:0, one launch (start us, length us, event | category | flops | bytes accessed | tf_op | source)
XLA Modules:
  0.0 41.9 jit_solution(4708401481271731860)
XLA Ops:
  0.6 38.6 %render_step.1 = (f32[62,16,256]{2,1,0:T(8,128)S(1)}, f32[62,16,256]{2,1,0:T(8,128)S(1)}, f32[62,16,256]{2,1,0:T(8,128)S(1)}, f32[62,16,256]{2,1,0:T(8,128)S(1)}, f32[1,1]{1,0:T(1,128)}) custom-call(f32[1,9]{1,0:T(1,128)} %camera_hbm.1, s32[1,1,16]{2,1,0:T(1,128)} %list_hbm.1, s32[1,1,8]{2,1,0:T(1,128)} %start_hbm.1, s32[1,1,8]{2,1,0:T(1,128)} %end_hbm.1, ...), custom_call_target="tpu_custom_call" | custom-call | tf_op jit(solution)/shard_map/render_step/pallas_call | solution.py:1053
  39.2 2.6 %adam_step.1 = (f32[62,16,256]{2,1,0:T(8,128)}, f32[62,16,256]{2,1,0:T(8,128)}, f32[62,16,256]{2,1,0:T(8,128)}, f32[62,16,256]{2,1,0:T(8,128)}, f32[1,1]{1,0:T(1,128)}) custom-call(f32[62,16,256]{2,1,0:T(8,128)S(1)} %get-tuple-element.15.grad_ref, f32[62,16,256]{2,1,0:T(8,128)S(1)} %get-tuple-element.16.gauss_ref, ...), custom_call_target="tpu_custom_call" | custom-call | tf_op jit(solution)/shard_map/adam_step/pallas_call | solution.py:1132

commit v5 on v4

--- a/solution.py
+++ b/solution.py
@@ -335,8 +335,10 @@
         fetch.start()
 
     def to_all(source, landing, length, phase):
-        for d_view in range(views_n):
-            for d_band in range(bands_n):
+        half = bands_n // 2
+        band_order = sorted(range(bands_n), key=lambda d: (d == 0, abs(d - half), d))
+        for d_view in range(views_n - 1, -1, -1):
+            for d_band in band_order:
                 if d_view + d_band == 0:
                     continue
                 peer = peer_band[d_band] * views_n + peer_view[d_view]

time: 42 us -> 41.2 us (0.981)
  Pallas kernels: 41.2 us -> 40.4 us
    pallas_call x1, Pallas kernels: 38.6 us -> 37.8 us  [per_device(): pl.pallas_call(functools.partial(step_kernel, geometry), out_shape=(kept,...]
where the time goes in v5:
time: 41.2 us; the launch traced here: 41 us
  Pallas kernels  40.4 us (98%)
  between operations  0.64 us (2%)
    pallas_call x1, Pallas kernels, per_device(): pl.pallas_call(functools.partial(step_kernel, geometry), out_shape=(kept,...  37.8 us
    pallas_call x1, Pallas kernels, per_device(): pl.pallas_call(adam_kernel, out_shape=(shape, shape, shape, shape, scalar...  2.62 us

profile of v5, /device:TPU:0, one launch (start us, length us, event | category | flops | bytes accessed | tf_op | source)
XLA Modules:
  0.0 41.0 jit_solution(738470858251600866)
XLA Ops:
  0.6 37.8 %render_step.1 = (f32[62,16,256]{2,1,0:T(8,128)S(1)}, f32[62,16,256]{2,1,0:T(8,128)S(1)}, f32[62,16,256]{2,1,0:T(8,128)S(1)}, f32[62,16,256]{2,1,0:T(8,128)S(1)}, f32[1,1]{1,0:T(1,128)}) custom-call(f32[1,9]{1,0:T(1,128)} %camera_hbm.1, s32[1,1,16]{2,1,0:T(1,128)} %list_hbm.1, s32[1,1,8]{2,1,0:T(1,128)} %start_hbm.1, s32[1,1,8]{2,1,0:T(1,128)} %end_hbm.1, ...), custom_call_target="tpu_custom_call" | custom-call | tf_op jit(solution)/shard_map/render_step/pallas_call | solution.py:1055
  38.4 2.6 %adam_step.1 = (f32[62,16,256]{2,1,0:T(8,128)}, f32[62,16,256]{2,1,0:T(8,128)}, f32[62,16,256]{2,1,0:T(8,128)}, f32[62,16,256]{2,1,0:T(8,128)}, f32[1,1]{1,0:T(1,128)}) custom-call(f32[62,16,256]{2,1,0:T(8,128)S(1)} %get-tuple-element.15.grad_ref, f32[62,16,256]{2,1,0:T(8,128)S(1)} %get-tuple-element.16.gauss_ref, ...), custom_call_target="tpu_custom_call" | custom-call | tf_op jit(solution)/shard_map/adam_step/pallas_call | solution.py:1134
